TPU v7x, 256 devices: a whole 4x4x8 slice. The times are simulated.
256 devices in a mesh: cam: 8 (over z), tm: 32 (over x, y, core).
Axes of the slice: x: 4, y: 4, z: 8, core: 2. Of those that a mesh axis runs over, the one named last changes fastest.
Arguments:
- embeds: bfloat16 [8, 4096, 2048], P(None, 'tm', 'cam'), may hold values from -6 to 6
- w_in: bfloat16 [2048, 2304], replicated, may hold values from -0.125 to 0.125
- log_decay: float32 [8, 32, 4096], P('cam', None, 'tm'), may hold values from -1 to 0, as said below
- clip_keep: float32 [32], replicated, may hold values from 0.55 to 0.8
- clip_starts: int32 [8, 3], P('cam'), may hold values from 1 to 4095
- valid_len: int32 [8], P('cam'), may hold values from 2048 to 4096, as said below
- norm_gain: float32 [2048], replicated, may hold values from 0.1 to 1.9
- g_out: bfloat16 [8, 4096, 2048], P('cam', 'tm'), may hold values from -6 to 6
Outputs:
- layer_out: bfloat16 [8, 4096, 2048], P('cam', 'tm')
- d_embeds: bfloat16 [8, 4096, 2048], P(None, 'tm', 'cam')
- d_w_in: float32 [2048, 2304], P(('cam', 'tm'))
Inputs may be any that keep to these rules, and one draw needn't show every extreme that they name: `log_decay`: negative. `valid_len`: some camera's valid length is 4096 in every draw.
All inputs are finite; a program needn't handle non-finite values.
Results may differ from a plain program's by a relative error of at most 0.014.
Values may be sent and summed in bfloat16 or wider, within the bound.
A program may use at most 128 MiB of HBM per device.

v0:
```python
import math

import jax
import jax.numpy as jnp
from jax import lax
from jax.sharding import PartitionSpec as P

D = 2048
H = 32
P_SIZE = 64
N = 128
Q = 128
HP = 2048


epsilon = 1e-05
precise = lax.Precision.HIGHEST


def entering(value, axis, combine, identity, reverse):
    size, position = (lax.axis_size(axis), lax.axis_index(axis))
    everything = jax.tree.map(lambda part: lax.all_gather(part, axis), value)
    start = jax.tree.map(
        lambda part, zero: jnp.broadcast_to(jnp.asarray(zero, part.dtype), part.shape),
        value,
        identity,
    )

    def hop(k, before):
        at = size - 1 - k if reverse else k
        reached = at > position if reverse else at < position
        new = combine(before, jax.tree.map(lambda part: part[at], everything))
        return jax.tree.map(lambda a, b: jnp.where(reached, a, b), new, before)

    return lax.fori_loop(0, size, hop, start)


def combine(earlier_item, later_item):
    return (
        earlier_item[0] * later_item[0],
        later_item[0][:, None, None] * earlier_item[1] + later_item[1],
    )


def grad_rows(x_rows, d_proj, grad_scale):

    def row_terms(first_row, row_count):
        return grad_scale * lax.dot_general(
            x_rows, d_proj, (((0,), (0,)), ((), ())), preferred_element_type=jnp.float32
        )

    return row_terms


def on_device(embeds, w_in, log_decay, clip_keep, clip_starts, valid_len, norm_gain, g_out):
    n_cam = lax.axis_size("cam")
    n_tm = lax.axis_size("tm")
    t_dev = embeds.shape[1]
    groups = t_dev // Q
    x_rows = lax.all_to_all(embeds, "cam", split_axis=0, concat_axis=2, tiled=True)[0]
    projected = jnp.dot(x_rows, w_in, preferred_element_type=jnp.float32).astype(jnp.bfloat16)
    positions = lax.axis_index("tm") * t_dev + jnp.arange(t_dev, dtype=jnp.int32)
    is_start = jnp.any(positions[:, None] == clip_starts[0][None, :], axis=1)
    log_rates = log_decay[0] + jnp.where(is_start[None, :], jnp.log(clip_keep)[:, None], 0.0)
    valid_rows = (positions < valid_len[0]).astype(jnp.float32)
    proj_float = projected.astype(jnp.float32)
    x_blocks = (proj_float[:, :HP].reshape(t_dev, H, P_SIZE) * valid_rows[:, None, None]).reshape(
        groups, Q, H, P_SIZE
    )
    b_blocks = proj_float[:, HP : HP + N].reshape(groups, Q, N)
    c_blocks = proj_float[:, HP + N :].reshape(groups, Q, N)
    cum_rate = jnp.cumsum(log_rates.reshape(H, groups, Q), axis=2).transpose(1, 0, 2)
    group_log = cum_rate[:, :, -1]
    causal = jnp.arange(Q)[:, None] >= jnp.arange(Q)[None, :]
    gaps = cum_rate[:, :, :, None] - cum_rate[:, :, None, :]
    weights = jnp.where(causal, jnp.exp(jnp.where(causal, gaps, 0.0)), 0.0)
    scores = jnp.einsum("ktn,ksn->kts", c_blocks, b_blocks, precision=precise)
    mixing = weights * scores[:, None]
    y_in = jnp.einsum("khts,kshp->kthp", mixing, x_blocks, precision=precise)
    tail_decay = jnp.exp(group_log[:, :, None] - cum_rate).transpose(0, 2, 1)
    lift_decay = jnp.exp(cum_rate).transpose(0, 2, 1)
    local_state = jnp.einsum(
        "kshp,ksn->khpn", x_blocks * tail_decay[:, :, :, None], b_blocks, precision=precise
    )
    zero_before = [jnp.zeros((H, P_SIZE, N), jnp.float32)]
    zero_end = jnp.exp(group_log[-1])[:, None, None] * zero_before[-1] + local_state[-1]
    dev_decay = jnp.exp(jnp.sum(group_log, axis=0))
    identity = (jnp.ones((H,), jnp.float32), jnp.zeros((H, P_SIZE, N), jnp.float32))
    s_in = entering((dev_decay, zero_end), "tm", combine, identity, False)[1]
    lead_log = jnp.cumsum(group_log, axis=0) - group_log
    state_before = jnp.exp(lead_log)[:, :, None, None] * s_in[None] + jnp.stack(zero_before)
    y_out = lift_decay[:, :, :, None] * jnp.einsum(
        "khpn,ktn->kthp", state_before, c_blocks, precision=precise
    )
    raw_out = (y_in + y_out).reshape(t_dev, H, P_SIZE)
    inv_rms = lax.rsqrt(jnp.mean(raw_out * raw_out, axis=-1, keepdims=True) + epsilon)
    normed = raw_out * inv_rms
    layer_out = (normed.reshape(t_dev, HP) * norm_gain[None, :] * valid_rows[:, None]).astype(
        jnp.bfloat16
    )
    d_normed = (g_out[0].astype(jnp.float32) * norm_gain[None, :] * valid_rows[:, None]).reshape(
        t_dev, H, P_SIZE
    )
    d_output = inv_rms * (d_normed - normed * jnp.mean(d_normed * normed, axis=-1, keepdims=True))
    d_blocks = d_output.reshape(groups, Q, H, P_SIZE)
    back_state = jnp.einsum(
        "kthp,ktn->khpn", d_blocks * lift_decay[:, :, :, None], c_blocks, precision=precise
    )
    zero_after = [jnp.zeros((H, P_SIZE, N), jnp.float32)]
    zero_start = jnp.exp(group_log[0])[:, None, None] * zero_after[0] + back_state[0]
    r_out = entering((dev_decay, zero_start), "tm", combine, identity, True)[1]
    trail_log = jnp.cumsum(group_log[::-1], axis=0)[::-1] - group_log
    grad_after = jnp.exp(trail_log)[:, :, None, None] * r_out[None] + jnp.stack(zero_after)
    d_inputs = jnp.einsum("khts,kthp->kshp", mixing, d_blocks, precision=precise)
    d_inputs = d_inputs + tail_decay[:, :, :, None] * jnp.einsum(
        "khpn,ksn->kshp", grad_after, b_blocks, precision=precise
    )
    pair_terms = weights * jnp.einsum("kthp,kshp->khts", d_blocks, x_blocks, precision=precise)
    d_c = jnp.einsum("khts,ksn->ktn", pair_terms, b_blocks, precision=precise)
    d_c = d_c + jnp.einsum(
        "kthp,khpn->ktn", d_blocks * lift_decay[:, :, :, None], state_before, precision=precise
    )
    d_b = jnp.einsum("khts,ktn->ksn", pair_terms, c_blocks, precision=precise)
    d_b = d_b + jnp.einsum(
        "kshp,khpn->ksn", x_blocks * tail_decay[:, :, :, None], grad_after, precision=precise
    )
    du_rows = d_inputs.reshape(t_dev, HP) * valid_rows[:, None]
    d_proj = jnp.concatenate(
        [du_rows, d_b.reshape(t_dev, N), d_c.reshape(t_dev, N)], axis=1
    ).astype(jnp.bfloat16)
    d_rows = lax.dot_general(
        d_proj, w_in, (((1,), (1,)), ((), ())), preferred_element_type=jnp.float32
    ).astype(jnp.bfloat16)
    d_embeds = lax.all_to_all(d_rows[None], "cam", split_axis=2, concat_axis=0, tiled=True)
    grad_scale = 1.0 / math.sqrt(n_cam * t_dev * n_tm)
    row_terms = grad_rows(x_rows, d_proj, grad_scale)
    d_w_in = lax.psum_scatter(
        row_terms(jnp.int32(0), lax.axis_size(("cam", "tm")) * (D // (n_cam * n_tm))),
        ("cam", "tm"),
        scatter_dimension=0,
        tiled=True,
    )
    return (layer_out[None], d_embeds, d_w_in)


def solution(mesh):
    return jax.shard_map(
        on_device,
        mesh=mesh,
        in_specs=(
            P(None, "tm", "cam"),
            P(),
            P("cam", None, "tm"),
            P(),
            P("cam", None),
            P("cam"),
            P(),
            P("cam", "tm", None),
        ),
        out_specs=(P("cam", "tm", None), P(None, "tm", "cam"), P(("cam", "tm"), None)),
        check_vma=False,
    )
```

profile of v0, /device:TPU:1, one launch (start us, length us, event | category | flops | bytes accessed | tf_op | source)
XLA Modules:
  0.0 852.8 jit_solution(4584384012298286301)
XLA Ops:
  7.2 2.1 copy.92
  9.3 9.0 %all-to-all-start = ((bf16[8,128,256]{1,2,0:T(8,128)(2,1)}), bf16[8,128,256]{1,2,0:T(8,128)(2,1)S(1)}, u32[]{:S(2)}, u32[]{:S(2)}) async-start(bf16[8,128,256]{1,2,0:T(8,128)(2,1)} %copy.92), calls=%async_computation | async-start | bytes 1048576 | tf_op jit(solution)/shard_map/all_to_all | solution.py:60
  20.1 16.1 %all-to-all-done = bf16[8,128,256]{1,2,0:T(8,128)(2,1)S(1)} async-done(((bf16[8,128,256]{1,2,0:T(8,128)(2,1)}), bf16[8,128,256]{1,2,0:T(8,128)(2,1)S(1)}, u32[]{:S(2)}, u32[]{:S(2)}) %all-to-all-start) | async-done | bytes 524320 | tf_op jit(solution)/shard_map/all_to_all | solution.py:60
  36.2 5.3 convolution_convert_fusion
  42.7 1.5 copy.98
  44.3 1.6 convolution_add_fusion.1
  47.4 22.6 %all-gather = f32[32,32,1]{1,2,0:T(1,128)S(1)} all-gather(f32[1,32,1]{1,2,0:T(1,128)S(1)} %get-tuple-element.310), channel_id=2, replica_groups=mesh['cam'=8,'tm'=32] {'tm'}, dimensions={0}, use_global_device_ids=true | all-gather | bytes 4224 | tf_op jit(solution)/shard_map/all_gather | solution.py:22
  73.5 6.5 fusion.8
  80.0 81.4 %all-gather.6.cloned.1.call-done = f32[1024,64,128]{2,1,0:T(8,128)} async-done(((f32[32,64,128]{2,1,0:T(8,128)}), f32[1024,64,128]{2,1,0:T(8,128)}) %all-gather.6.cloned.1.call-update) | async-done | bytes 33554448 | tf_op jit(solution)/shard_map/all_gather | solution.py:22
  161.4 48.1 %while.30 = (s32[]{:T(128)}, f32[32,64,128]{2,1,0:T(8,128)S(1)}, s32[]{:T(128)}, f32[32,32]{1,0:T(8,128)S(1)}, f32[32,32,64,128]{3,2,1,0:T(8,128)}, /*index=5*/s32[]{:T(128)}, s32[]{:T(128)}) while((s32[]{:T(128)}, f32[32,64,128]{2,1,0:T(8,128)S(1)}, s32[]{:T(128)}, f32[32,32]{1,0:T(8,128)S(1)}, f32[32,32,64,128]{3,2,1,0:T(8,128)}, ...), condition=%wide.region_3.4_spmd.clone, body=%wide.region_2.3_spmd.clone.sunk | while | flops 1048580 | bytes 3146225 | solution.py:35
  209.6 2.0 fusion.24
  213.5 2.4 convolution_add_fusion
  216.1 3.3 convolution_bitcast_fusion
  219.4 4.0 multiply_reduce_fusion
  224.4 3.4 fusion.11
  227.8 106.3 %all-gather.8.cloned.1.call-done = f32[1024,64,128]{2,1,0:T(8,128)} async-done(((f32[32,64,128]{2,1,0:T(8,128)}), f32[1024,64,128]{2,1,0:T(8,128)}) %all-gather.8.cloned.1.call-update) | async-done | bytes 33554448 | tf_op jit(solution)/shard_map/all_gather | solution.py:22
  334.1 48.5 %while.31 = (s32[]{:T(128)}, f32[32,64,128]{2,1,0:T(8,128)S(1)}, s32[]{:T(128)}, f32[32,32]{1,0:T(8,128)S(1)}, f32[32,32,64,128]{3,2,1,0:T(8,128)}, /*index=5*/s32[]{:T(128)}, s32[]{:T(128)}, s32[]{:T(128)}, s32[]{:T(128)}) while((s32[]{:T(128)}, f32[32,64,128]{2,1,0:T(8,128)S(1)}, s32[]{:T(128)}, f32[32,32]{1,0:T(8,128)S(1)}, ...), condition=%wide.region_7.8_spmd.clone, body=%wide.region_6.7_spmd.clone.sunk | while | flops 1048584 | bytes 3146287 | solution.py:35
  334.1 1.5 fusion.81
  340.2 1.5 fusion.81
  341.8 1.5 fusion.81
  343.3 1.5 fusion.81
  382.7 1.9 convolution_bitcast_fusion.1
  385.6 2.4 fusion.17
  388.0 1.6 copy.104
  389.8 7.9 multiply_bitcast_fusion
  397.6 18.7 %copy.118 = f32[2048,2304]{1,0:T(8,128)} copy(f32[2048,2304]{0,1:T(8,128)} %multiply_bitcast_fusion) | data formatting | bytes 37748736
  416.3 6.8 fusion.2
  424.4 11.5 %reduce.2 = bf16[2048,128]{1,0:T(8,128)(2,1)S(1)} reduce(bf16[2048,1,128]{2,1,0:T(2,128)(2,1)S(1)} %bitcast.139, bf16[]{:T(256)} %broadcast.264), dimensions={1}, to_apply=%bitcast.109.reduce_sub_computation | reduce | bytes 1048578
  436.9 6.7 all-to-all-start.1
  445.3 16.4 %all-to-all-done.1 = bf16[8,2,16384]{2,1,0:T(2,128)(2,1)} async-done(((bf16[8,2,16384]{2,1,0:T(2,128)(2,1)}), bf16[8,2,16384]{2,1,0:T(2,128)(2,1)}, u32[]{:S(2)}, u32[]{:S(2)}) %all-to-all-start.1) | async-done | bytes 524320 | tf_op jit(solution)/shard_map/all_to_all | solution.py:134
  461.7 2.2 reshape.430
  465.0 381.3 %reduce-scatter.4.cloned.1.call-done = f32[8,2304]{1,0:T(8,128)} async-done(((f32[2048,2304]{1,0:T(8,128)}), f32[8,2304]{1,0:T(8,128)}) %reduce-scatter.4.cloned.1.call-update) | async-done | bytes 73744
  (195 shorter events, 104.7 us)
Async XLA Ops:
  7.2 11.1 %copy-start.11 = (f32[32]{0:T(128)S(1)}, f32[32]{0:T(128)}, u32[]{:S(2)}) copy-start(f32[32]{0:T(128)} %param.15) | copy-start | bytes 388
  7.2 11.8 %copy-start.12 = (s32[1,3]{1,0:T(1,128)S(1)}, s32[1,3]{1,0:T(1,128)}, u32[]{:S(2)}) copy-start(s32[1,3]{1,0:T(1,128)} %param.16) | copy-start | bytes 40
  7.2 11.9 %copy-start.10 = (f32[1,32,128]{2,1,0:T(8,128)S(1)}, f32[1,32,128]{2,1,0:T(8,128)}, u32[]{:S(2)}) copy-start(f32[1,32,128]{2,1,0:T(8,128)} %param.14) | copy-start | bytes 49156
  9.3 27.0 %all-to-all-start = ((bf16[8,128,256]{1,2,0:T(8,128)(2,1)}), bf16[8,128,256]{1,2,0:T(8,128)(2,1)S(1)}, u32[]{:S(2)}, u32[]{:S(2)}) async-start(bf16[8,128,256]{1,2,0:T(8,128)(2,1)} %copy.92), calls=%async_computation | async-start | bytes 1048576 | tf_op jit(solution)/shard_map/all_to_all | solution.py:60
  18.3 143.2 %all-gather.6.cloned.1.call-start = ((), (), s32[]{:S(2)}) async-start(), calls=%async_computation.3 | async-start | bytes 34603008 | tf_op jit(solution)/shard_map/all_gather | solution.py:22
  36.2 5.3 copy-start.4
  41.5 2.8 copy-start.6
  44.3 1.7 copy-start
  44.3 3.1 copy-start.9
  46.0 288.1 %all-gather.8.cloned.1.call-start = ((), (), s32[]{:S(2)}) async-start(), calls=%async_computation.4 | async-start | bytes 34603008 | tf_op jit(solution)/shard_map/all_gather | solution.py:22
  212.5 1.0 copy-start.2
  215.9 630.4 %reduce-scatter.4.cloned.1.call-start = ((), (), s32[]{:S(2)}) async-start(), calls=%async_computation.5 | async-start | bytes 18948096
  216.1 3.3 copy-start.3
  216.1 3.3 copy-start.7
  334.1 48.6 %copy-start.1 = (f32[128,2048]{0,1:T(8,128)S(1)}, f32[128,2048]{0,1:T(8,128)}, u32[]{:S(2)}) copy-start(f32[128,2048]{0,1:T(8,128)} %copy-done) | copy-start | bytes 3145732
  382.6 2.9 copy-start.8
  388.0 1.8 copy-start.5
  436.9 24.8 %all-to-all-start.1 = ((bf16[8,2,16384]{2,1,0:T(2,128)(2,1)}), bf16[8,2,16384]{2,1,0:T(2,128)(2,1)}, u32[]{:S(2)}, u32[]{:S(2)}) async-start(bf16[8,2,16384]{2,1,0:T(2,128)(2,1)} %reshape.429), calls=%async_computation.1 | async-start | bytes 1048576 | tf_op jit(solution)/shard_map/all_to_all | solution.py:134
Sparse Core Ops, SparseCore 0:
  46.1 115.3 all-gather.5
  216.0 118.0 all-gather.7
  416.4 429.8 reduce-scatter.3
where the time goes:
time: 861 us; the launch traced here: 853 us
  waiting for transfers between devices  602 us (70%)
  other arithmetic  110 us (13%)
  matrix products  50.3 us (6%)
  local copies, waits for them, and re-layouts  35.1 us (4%)
  blocking collectives  22.6 us (3%)
  starting transfers between devices  16 us (2%)
  between operations  14.8 us (2%)
    unnamed x4, waiting for transfers between devices  381 us
    all_gather x2, waiting for transfers between devices, entering(): everything = jax.tree.map(lambda part: lax.all_gather(part, axis), value)  188 us
    select_n x64, other arithmetic, hop(): return jax.tree.map(lambda a, b: jnp.where(reached, a, b), new, before)  93.7 us
    unnamed x33, local copies, waits for them, and re-layouts  26.5 us
    all_gather x1, blocking collectives, entering(): everything = jax.tree.map(lambda part: lax.all_gather(part, axis), value)  22.6 us
  transfers between devices with their start and end apart: 5, of which 5 were waited for; matrix products, arithmetic and copies ran while one was open for 6% of the time, Pallas kernels for 0%

commit v1 on v0

--- a/solution.py
+++ b/solution.py
@@ -17,39 +17,25 @@
 precise = lax.Precision.HIGHEST
 
 
-def entering(value, axis, combine, identity, reverse):
-    size, position = (lax.axis_size(axis), lax.axis_index(axis))
-    everything = jax.tree.map(lambda part: lax.all_gather(part, axis), value)
-    start = jax.tree.map(
-        lambda part, zero: jnp.broadcast_to(jnp.asarray(zero, part.dtype), part.shape),
-        value,
-        identity,
-    )
-
-    def hop(k, before):
-        at = size - 1 - k if reverse else k
-        reached = at > position if reverse else at < position
-        new = combine(before, jax.tree.map(lambda part: part[at], everything))
-        return jax.tree.map(lambda a, b: jnp.where(reached, a, b), new, before)
-
-    return lax.fori_loop(0, size, hop, start)
-
-
-def combine(earlier_item, later_item):
-    return (
-        earlier_item[0] * later_item[0],
-        later_item[0][:, None, None] * earlier_item[1] + later_item[1],
-    )
-
-
-def grad_rows(x_rows, d_proj, grad_scale):
-
-    def row_terms(first_row, row_count):
-        return grad_scale * lax.dot_general(
-            x_rows, d_proj, (((0,), (0,)), ((), ())), preferred_element_type=jnp.float32
-        )
-
-    return row_terms
+def prefix_states(block_log, state, reverse):
+    size = lax.axis_size("tm")
+    extra = jnp.broadcast_to(block_log[:, None, None], (H, 8, N))
+    packed = jnp.concatenate([state, extra], axis=1)
+    mine = lax.all_to_all(packed, "tm", split_axis=0, concat_axis=0, tiled=True)
+    logs = mine[:, P_SIZE, 0]
+    parts = mine[:, :P_SIZE].reshape(size, P_SIZE * N)
+    cum = jnp.cumsum(logs)
+    at = jnp.arange(size)
+    if reverse:
+        reach = at[None, :] > at[:, None]
+        gap = (cum - logs)[None, :] - cum[:, None]
+    else:
+        reach = at[None, :] < at[:, None]
+        gap = (cum - logs)[:, None] - cum[None, :]
+    factors = jnp.where(reach, jnp.exp(jnp.where(reach, gap, 0.0)), 0.0)
+    entered = jnp.dot(factors, parts, precision=precise).astype(jnp.bfloat16)
+    entered = entered.reshape(size, P_SIZE, N)
+    return lax.all_to_all(entered, "tm", split_axis=0, concat_axis=0, tiled=True).astype(jnp.float32)
 
 
 def on_device(embeds, w_in, log_decay, clip_keep, clip_starts, valid_len, norm_gain, g_out):
@@ -84,9 +70,8 @@
     )
     zero_before = [jnp.zeros((H, P_SIZE, N), jnp.float32)]
     zero_end = jnp.exp(group_log[-1])[:, None, None] * zero_before[-1] + local_state[-1]
-    dev_decay = jnp.exp(jnp.sum(group_log, axis=0))
-    identity = (jnp.ones((H,), jnp.float32), jnp.zeros((H, P_SIZE, N), jnp.float32))
-    s_in = entering((dev_decay, zero_end), "tm", combine, identity, False)[1]
+    block_log = jnp.sum(group_log, axis=0)
+    s_in = prefix_states(block_log, zero_end, False)
     lead_log = jnp.cumsum(group_log, axis=0) - group_log
     state_before = jnp.exp(lead_log)[:, :, None, None] * s_in[None] + jnp.stack(zero_before)
     y_out = lift_decay[:, :, :, None] * jnp.einsum(
@@ -108,7 +93,7 @@
     )
     zero_after = [jnp.zeros((H, P_SIZE, N), jnp.float32)]
     zero_start = jnp.exp(group_log[0])[:, None, None] * zero_after[0] + back_state[0]
-    r_out = entering((dev_decay, zero_start), "tm", combine, identity, True)[1]
+    r_out = prefix_states(block_log, zero_start, True)
     trail_log = jnp.cumsum(group_log[::-1], axis=0)[::-1] - group_log
     grad_after = jnp.exp(trail_log)[:, :, None, None] * r_out[None] + jnp.stack(zero_after)
     d_inputs = jnp.einsum("khts,kthp->kshp", mixing, d_blocks, precision=precise)
@@ -128,18 +113,17 @@
     d_proj = jnp.concatenate(
         [du_rows, d_b.reshape(t_dev, N), d_c.reshape(t_dev, N)], axis=1
     ).astype(jnp.bfloat16)
-    d_rows = lax.dot_general(
-        d_proj, w_in, (((1,), (1,)), ((), ())), preferred_element_type=jnp.float32
-    ).astype(jnp.bfloat16)
-    d_embeds = lax.all_to_all(d_rows[None], "cam", split_axis=2, concat_axis=0, tiled=True)
+    all_proj = lax.all_gather(d_proj, "cam").reshape(n_cam * t_dev, HP + 2 * N)
+    width = D // n_cam
+    w_mine = lax.dynamic_slice_in_dim(w_in, lax.axis_index("cam") * width, width, axis=0)
+    d_embeds = lax.dot_general(
+        all_proj, w_mine, (((1,), (1,)), ((), ())), preferred_element_type=jnp.float32
+    ).astype(jnp.bfloat16).reshape(n_cam, t_dev, width)
     grad_scale = 1.0 / math.sqrt(n_cam * t_dev * n_tm)
-    row_terms = grad_rows(x_rows, d_proj, grad_scale)
-    d_w_in = lax.psum_scatter(
-        row_terms(jnp.int32(0), lax.axis_size(("cam", "tm")) * (D // (n_cam * n_tm))),
-        ("cam", "tm"),
-        scatter_dimension=0,
-        tiled=True,
+    row_terms = grad_scale * lax.dot_general(
+        embeds.reshape(n_cam * t_dev, width), all_proj, (((0,), (0,)), ((), ())), preferred_element_type=jnp.float32
     )
+    d_w_in = lax.psum_scatter(row_terms, "tm", scatter_dimension=0, tiled=True)
     return (layer_out[None], d_embeds, d_w_in)
 
 

time: 861 us -> 302 us (0.35)
  waiting for transfers between devices: 602 us -> 181 us
  other arithmetic: 110 us -> 8.47 us
  blocking collectives: 22.6 us -> 0 us
  local copies, waits for them, and re-layouts: 35.1 us -> 17 us
  starting transfers between devices: 16 us -> 32.1 us
    unnamed x4 -> x3, waiting for transfers between devices: 381 us -> 77.7 us
    all_gather x2 -> x1, waiting for transfers between devices: 188 us -> 51.8 us  [on_device(): all_proj = lax.all_gather(d_proj, 'cam').reshape(n_cam * t_dev, HP + 2 * N)]
    select_n x64 -> x0, other arithmetic: 93.7 us -> none  [hop(): return jax.tree.map(lambda a, b: jnp.where(reached, a, b), new, before)]
    all_gather x1 -> x0, blocking collectives: 22.6 us -> none  [entering(): everything = jax.tree.map(lambda part: lax.all_gather(part, axis), value)]
    unnamed x33 -> x18, local copies, waits for them, and re-layouts: 26.5 us -> 5.9 us
    all_to_all x1 -> x4, waiting for transfers between devices: 16.4 us -> 35.8 us  [the longest x2 30.3 us: prefix_states(): mine = lax.all_to_all(packed, 'tm', split_axis=0, concat_axis=0, tiled=True)]
    all_to_all x1 -> x4, starting transfers between devices: 6.73 us -> 23.1 us  [the longest x2 13.9 us: prefix_states(): mine = lax.all_to_all(packed, 'tm', split_axis=0, concat_axis=0, tiled=True)]
    unnamed x3 -> x0, other arithmetic: 11.5 us -> none
  transfers between devices with their start and end apart: 5 -> 7, of which waited for: 5 -> 7; matrix products, arithmetic and copies ran while one was open for 6% -> 11% of each run, Pallas kernels for 0% -> 0%
where the time goes in v1:
time: 302 us; the launch traced here: 300 us
  waiting for transfers between devices  181 us (60%)
  matrix products  46 us (15%)
  starting transfers between devices  32.1 us (11%)
  local copies, waits for them, and re-layouts  17 us (6%)
  between operations  15.1 us (5%)
  other arithmetic  8.47 us (3%)
    unnamed x3, waiting for transfers between devices  77.7 us
    all_gather x1, waiting for transfers between devices, on_device(): all_proj = lax.all_gather(d_proj, 'cam').reshape(n_cam * t_dev, HP + 2 * N)  51.8 us
    all_to_all x2, waiting for transfers between devices, prefix_states(): mine = lax.all_to_all(packed, 'tm', split_axis=0, concat_axis=0, tiled=True)  30.3 us
    all_to_all x1, waiting for transfers between devices, on_device(): lax.all_to_all(embeds, 'cam', split_axis=0, concat_axis=2, tiled=True)[0]  16.1 us
    all_to_all x2, starting transfers between devices, prefix_states(): mine = lax.all_to_all(packed, 'tm', split_axis=0, concat_axis=0, tiled=True)  13.9 us
    all_to_all x2, starting transfers between devices, prefix_states(): lax.all_to_all(entered, 'tm', split_axis=0, concat_axis=0, tiled=True)  9.21 us
    all_to_all x1, starting transfers between devices, on_device(): lax.all_to_all(embeds, 'cam', split_axis=0, concat_axis=2, tiled=True)[0]  9 us
    dot_general x1, matrix products, on_device(): y_in = jnp.einsum('khts,kshp->kthp', mixing, x_blocks, precision=precise)  6.51 us
  transfers between devices with their start and end apart: 7, of which 7 were waited for; matrix products, arithmetic and copies ran while one was open for 11% of the time, Pallas kernels for 0%

profile of v1, /device:TPU:1, one launch (start us, length us, event | category | flops | bytes accessed | tf_op | source)
XLA Modules:
  0.0 300.0 jit_solution(2047633472301824590)
XLA Ops:
  7.2 2.1 copy.62
  9.3 9.0 %all-to-all-start = ((bf16[8,128,256]{1,2,0:T(8,128)(2,1)}), bf16[8,128,256]{1,2,0:T(8,128)(2,1)S(1)}, u32[]{:S(2)}, u32[]{:S(2)}) async-start(bf16[8,128,256]{1,2,0:T(8,128)(2,1)} %copy.62), calls=%async_computation | async-start | bytes 1048576 | tf_op jit(solution)/shard_map/all_to_all | solution.py:46
  20.1 16.1 %all-to-all-done = bf16[8,128,256]{1,2,0:T(8,128)(2,1)S(1)} async-done(((bf16[8,128,256]{1,2,0:T(8,128)(2,1)}), bf16[8,128,256]{1,2,0:T(8,128)(2,1)S(1)}, u32[]{:S(2)}, u32[]{:S(2)}) %all-to-all-start) | async-done | bytes 524320 | tf_op jit(solution)/shard_map/all_to_all | solution.py:46
  36.2 5.1 %convolution_convert_fusion.2 = bf16[128,2304]{1,0:T(8,128)(2,1)S(1)} fusion(bf16[128,2048]{0,1:T(8,128)(2,1)S(1)} %bitcast.133, bf16[2048,2304]{1,0:T(8,128)(2,1)} %param.9), kind=kOutput, calls=%fused_computation.5 | convolution fusion | flops 1208254464 | bytes 10551296 | tf_op jit(solution)/shard_map/dot_general | solution.py:47
  43.7 7.8 %all-to-all-start.1 = ((f32[32,72,128]{2,1,0:T(8,128)}), f32[32,72,128]{2,1,0:T(8,128)}, u32[]{:S(2)}, u32[]{:S(2)}) async-start(f32[32,72,128]{2,1,0:T(8,128)} %pad_maximum_fusion.1), calls=%async_computation.1 | async-start | bytes 2359296 | tf_op jit(solution)/shard_map/all_to_all | solution.py:24
  51.5 1.2 copy.69
  52.8 17.1 %all-to-all-done.1 = f32[32,72,128]{2,1,0:T(8,128)} async-done(((f32[32,72,128]{2,1,0:T(8,128)}), f32[32,72,128]{2,1,0:T(8,128)}, u32[]{:S(2)}, u32[]{:S(2)}) %all-to-all-start.1) | async-done | bytes 1179680 | tf_op jit(solution)/shard_map/all_to_all | solution.py:24
  69.9 1.2 slice_reduce_fusion.2
  71.3 1.3 slice.41
  72.6 1.6 fusion.17
  75.1 4.6 %all-to-all-start.2 = ((bf16[32,64,128]{2,1,0:T(8,128)(2,1)}), bf16[32,64,128]{2,1,0:T(8,128)(2,1)}, u32[]{:S(2)}, u32[]{:S(2)}) async-start(bf16[32,64,128]{2,1,0:T(8,128)(2,1)} %bitcast.135), calls=%async_computation.2 | async-start | bytes 1048576 | tf_op jit(solution)/shard_map/all_to_all | solution.py:38
  80.8 2.6 copy.63
  83.5 6.5 %fusion.7 = f32[1,128,32,64]{1,3,2,0:T(8,128)} fusion(f32[128,128]{1,0:T(8,128)S(1)} %fusion.65, f32[32,128]{1,0:T(8,128)S(1)} %bitcast.139, pred[128,128]{1,0:T(8,128)(4,1)S(1)} %iota_compare_fusion, f32[128,32,64]{0,2,1:T(8,128)} %bitcast.136, f32[128]{0:T(128)S(1)} %compare_convert_fusion), kind=kOutput, calls=%fused_computation.13 | convolution fusion | flops 405012480 | bytes 2195968 | tf_op jit(solution)/shard_map/khts,kshp->kthp/dot_general | solution.py:65
  91.2 2.2 fusion.32
  93.9 1.6 subtract_multiply_fusion
  95.5 1.4 convolution_add_fusion
  98.0 6.1 %all-to-all-start.3 = ((f32[32,72,128]{2,1,0:T(8,128)}), f32[32,72,128]{2,1,0:T(8,128)}, u32[]{:S(2)}, u32[]{:S(2)}) async-start(f32[32,72,128]{2,1,0:T(8,128)} %pad_maximum_fusion), calls=%async_computation.3 | async-start | bytes 2359296 | tf_op jit(solution)/shard_map/all_to_all | solution.py:24
  104.1 5.2 %multiply_reduce_fusion = f32[128,128]{1,0:T(8,128)S(1)} fusion(f32[1,128,32,64]{1,3,2,0:T(8,128)S(1)} %subtract_multiply_fusion, f32[32,128]{1,0:T(8,128)S(1)} %bitcast.140, pred[128,128]{1,0:T(8,128)(4,1)S(1)} %iota_compare_fusion, f32[128,32,64]{0,2,1:T(8,128)} %bitcast.137, f32[128]{0:T(128)S(1)} %compare_convert_fusion), kind=kOutput, calls=%fused_computation.6 | convolution fusion | flops 405520384 | bytes 2195968 | tf_op jit(solution)/shard_map/kthp,kshp->khts/dot_general | solution.py:103
  109.3 13.3 %all-to-all-done.3 = f32[32,72,128]{2,1,0:T(8,128)} async-done(((f32[32,72,128]{2,1,0:T(8,128)}), f32[32,72,128]{2,1,0:T(8,128)}, u32[]{:S(2)}, u32[]{:S(2)}) %all-to-all-start.3) | async-done | bytes 1179680 | tf_op jit(solution)/shard_map/all_to_all | solution.py:24
  123.9 1.3 slice.43
  125.3 1.6 fusion.18
  127.8 4.6 %all-to-all-start.4 = ((bf16[32,64,128]{2,1,0:T(8,128)(2,1)}), bf16[32,64,128]{2,1,0:T(8,128)(2,1)}, u32[]{:S(2)}, u32[]{:S(2)}) async-start(bf16[32,64,128]{2,1,0:T(8,128)(2,1)} %bitcast.134), calls=%async_computation.4 | async-start | bytes 1048576 | tf_op jit(solution)/shard_map/all_to_all | solution.py:38
  132.4 3.0 convolution_bitcast_fusion.1
  136.4 3.4 %fusion.10 = f32[1,128,32,64]{1,3,2,0:T(8,128)} fusion(f32[1,128,32,64]{1,3,2,0:T(8,128)S(1)} %subtract_multiply_fusion, f32[128,128]{1,0:T(8,128)S(1)} %fusion.65, f32[32,128]{1,0:T(8,128)S(1)} %bitcast.141, pred[128,128]{1,0:T(8,128)(4,1)S(1)} %iota_compare_fusion), kind=kOutput, calls=%fused_computation.14 | convolution fusion | flops 404750336 | bytes 2195456 | tf_op jit(solution)/shard_map/khts,kthp->kshp/dot_general | solution.py:99
  139.7 4.3 %all-to-all-done.4 = bf16[32,64,128]{2,1,0:T(8,128)(2,1)} async-done(((bf16[32,64,128]{2,1,0:T(8,128)(2,1)}), bf16[32,64,128]{2,1,0:T(8,128)(2,1)}, u32[]{:S(2)}, u32[]{:S(2)}) %all-to-all-start.4) | async-done | bytes 524320 | tf_op jit(solution)/shard_map/all_to_all | solution.py:38
  144.0 2.9 convolution_bitcast_fusion.2
  148.0 1.8 fusion.16
  151.2 51.8 %all-gather.2.cloned.1.call-done = bf16[8,128,2304]{2,1,0:T(8,128)(2,1)} async-done(((bf16[1,128,2304]{2,1,0:T(8,128)(2,1)}), bf16[8,128,2304]{2,1,0:T(8,128)(2,1)}) %all-gather.2.cloned.1.call-update) | async-done | bytes 4718608 | tf_op jit(solution)/shard_map/all_gather | solution.py:116
  203.0 3.9 %fusion.1 = f32[256,2304]{0,1:T(8,128)S(1)} fusion(bf16[8,128,2304]{2,1,0:T(8,128)(2,1)} %all-gather.2.cloned.1.call-done, bf16[8,128,256]{2,1,0:T(8,128)(2,1)} %param.8), kind=kOutput, calls=%fused_computation.4 | convolution fusion | flops 1208549376 | bytes 7602176 | tf_op jit(solution)/shard_map/dot_general | solution.py:123
  206.9 2.0 copy.86
  210.6 4.9 %convolution_convert_fusion.3 = bf16[1024,256]{1,0:T(8,128)(2,1)} fusion(bf16[1024,2304]{1,0:T(8,128)(2,1)} %bitcast.144, bf16[2048,2304]{1,0:T(8,128)(2,1)} %param.9, s32[]{:T(128)S(6)} %select_n.49), kind=kOutput, calls=%fused_computation.23 | convolution fusion | flops 1208221696 | bytes 6422532 | tf_op jit(solution)/shard_map/dot_general | solution.py:119
  215.5 77.7 %reduce-scatter.4.cloned.1.call-done = f32[8,2304]{1,0:T(8,128)} async-done(((f32[256,2304]{1,0:T(8,128)}), f32[8,2304]{1,0:T(8,128)}) %reduce-scatter.4.cloned.1.call-update) | async-done | bytes 73744
  (61 shorter events, 16.1 us)
Async XLA Ops:
  7.2 11.1 %copy-start.5 = (s32[1,3]{1,0:T(1,128)S(1)}, s32[1,3]{1,0:T(1,128)}, u32[]{:S(2)}) copy-start(s32[1,3]{1,0:T(1,128)} %param.12) | copy-start | bytes 40
  7.2 11.2 %copy-start.6 = (f32[32]{0:T(128)S(1)}, f32[32]{0:T(128)}, u32[]{:S(2)}) copy-start(f32[32]{0:T(128)} %param.11) | copy-start | bytes 388
  7.2 11.8 %copy-start.4 = (f32[1,32,128]{2,1,0:T(8,128)S(1)}, f32[1,32,128]{2,1,0:T(8,128)}, u32[]{:S(2)}) copy-start(f32[1,32,128]{2,1,0:T(8,128)} %param.10) | copy-start | bytes 49156
  9.3 27.0 %all-to-all-start = ((bf16[8,128,256]{1,2,0:T(8,128)(2,1)}), bf16[8,128,256]{1,2,0:T(8,128)(2,1)S(1)}, u32[]{:S(2)}, u32[]{:S(2)}) async-start(bf16[8,128,256]{1,2,0:T(8,128)(2,1)} %copy.62), calls=%async_computation | async-start | bytes 1048576 | tf_op jit(solution)/shard_map/all_to_all | solution.py:46
  41.3 42.1 %copy-start.1 = (bf16[128,2304]{1,0:T(8,128)(2,1)}, bf16[128,2304]{1,0:T(8,128)(2,1)S(1)}, u32[]{:S(2)}) copy-start(bf16[128,2304]{1,0:T(8,128)(2,1)S(1)} %convolution_convert_fusion.2) | copy-start | bytes 1769476
  43.7 9.0 %copy-start.3 = (f32[2048]{0:T(1024)S(1)}, f32[2048]{0:T(1024)}, u32[]{:S(2)}) copy-start(f32[2048]{0:T(1024)} %param.14) | copy-start | bytes 24580
  43.7 26.2 %all-to-all-start.1 = ((f32[32,72,128]{2,1,0:T(8,128)}), f32[32,72,128]{2,1,0:T(8,128)}, u32[]{:S(2)}, u32[]{:S(2)}) async-start(f32[32,72,128]{2,1,0:T(8,128)} %pad_maximum_fusion.1), calls=%async_computation.1 | async-start | bytes 2359296 | tf_op jit(solution)/shard_map/all_to_all | solution.py:24
  52.7 40.7 %copy-start = (f32[1,128,2048]{1,2,0:T(8,128)}, f32[1,128,2048]{1,2,0:T(8,128)S(1)}, u32[]{:S(2)}) copy-start(f32[1,128,2048]{1,2,0:T(8,128)S(1)} %copy.69) | copy-start | bytes 3145732
  75.1 16.1 %all-to-all-start.2 = ((bf16[32,64,128]{2,1,0:T(8,128)(2,1)}), bf16[32,64,128]{2,1,0:T(8,128)(2,1)}, u32[]{:S(2)}, u32[]{:S(2)}) async-start(bf16[32,64,128]{2,1,0:T(8,128)(2,1)} %bitcast.135), calls=%async_computation.2 | async-start | bytes 1048576 | tf_op jit(solution)/shard_map/all_to_all | solution.py:38
  98.0 24.5 %all-to-all-start.3 = ((f32[32,72,128]{2,1,0:T(8,128)}), f32[32,72,128]{2,1,0:T(8,128)}, u32[]{:S(2)}, u32[]{:S(2)}) async-start(f32[32,72,128]{2,1,0:T(8,128)} %pad_maximum_fusion), calls=%async_computation.3 | async-start | bytes 2359296 | tf_op jit(solution)/shard_map/all_to_all | solution.py:24
  127.8 16.3 %all-to-all-start.4 = ((bf16[32,64,128]{2,1,0:T(8,128)(2,1)}), bf16[32,64,128]{2,1,0:T(8,128)(2,1)}, u32[]{:S(2)}, u32[]{:S(2)}) async-start(bf16[32,64,128]{2,1,0:T(8,128)(2,1)} %bitcast.134), calls=%async_computation.4 | async-start | bytes 1048576 | tf_op jit(solution)/shard_map/all_to_all | solution.py:38
  132.4 70.6 %all-gather.2.cloned.1.call-start = ((), (), s32[]{:S(2)}) async-start(), calls=%async_computation.6 | async-start | bytes 5308416 | tf_op jit(solution)/shard_map/all_gather | solution.py:116
  139.7 8.3 %copy-start.2 = (f32[1,128,32,64]{1,3,2,0:T(8,128)S(1)}, f32[1,128,32,64]{1,3,2,0:T(8,128)}, u32[]{:S(2)}) copy-start(f32[1,128,32,64]{1,3,2,0:T(8,128)} %fusion.10) | copy-start | bytes 3145732
  151.1 142.0 %reduce-scatter.4.cloned.1.call-start = ((), (), s32[]{:S(2)}) async-start(), calls=%async_computation.7 | async-start | bytes 2433024
Sparse Core Ops, SparseCore 0:
  151.3 51.6 all-gather.1
  209.0 84.1 reduce-scatter.3

commit v2 on v1

--- a/solution.py
+++ b/solution.py
@@ -1,8 +1,11 @@
+import functools
 import math
 
 import jax
 import jax.numpy as jnp
 from jax import lax
+from jax.experimental import pallas as pl
+from jax.experimental.pallas import tpu as pltpu
 from jax.sharding import PartitionSpec as P
 
 D = 2048
@@ -15,6 +18,8 @@
 
 epsilon = 1e-05
 precise = lax.Precision.HIGHEST
+MESH = pl.DeviceIdType.MESH
+NX, NY, NZ = 4, 4, 8
 
 
 def prefix_states(block_log, state, reverse):
@@ -38,6 +43,199 @@
     return lax.all_to_all(entered, "tm", split_axis=0, concat_axis=0, tiled=True).astype(jnp.float32)
 
 
+def place():
+    tm = lax.axis_index("tm")
+    return tm // (2 * NY), (tm // 2) % NY, lax.axis_index("cam"), tm % 2
+
+
+def at(x, y, z, core):
+    return (z, (x * NY + y) * 2 + core)
+
+
+def greet(peers):
+    barrier = pltpu.get_barrier_semaphore()
+    for peer in peers:
+        pl.semaphore_signal(barrier, inc=1, device_id=peer, device_id_type=MESH)
+    pl.semaphore_wait(barrier, len(peers))
+
+
+def send(src, dst, sem_a, sem_b, peer):
+    return pltpu.make_async_remote_copy(
+        src_ref=src, dst_ref=dst, send_sem=sem_a, recv_sem=sem_b, device_id=peer, device_id_type=MESH
+    )
+
+
+def grad_kernel(scale, dp_ref, xt_ref, w_ref, emb_ref, dw_ref, wv, xg, pg, rows, s2, r2, s3, r3, own,
+                w_sem, x_send, x_recv, p_send, p_recv, e_send, e_recv, send2, recv2, send3, recv3):
+    x, y, z, core = place()
+    half = dp_ref.shape[1] // 2
+    width = wv.shape[1]
+    t = dp_ref.shape[0]
+    for j in range(NZ):
+        c = (z + 1 + j) % NZ
+        pltpu.make_async_copy(w_ref.at[pl.ds(pl.multiple_of(c * width, width), width)], wv.at[j], w_sem.at[j]).start()
+    peers = []
+    for j in range(1, NX):
+        peers += [at((x + j) % NX, y, z, core), at((x + j) % NX, y, z, 1 - core)]
+    for j in range(1, NY):
+        peers += [at(x, (y + j) % NY, z, core), at(x, (y + j) % NY, z, 1 - core)]
+    for j in range(1, NZ):
+        peers += [at(x, y, (z + j) % NZ, core), at(x, y, (z + j) % NZ, 1 - core)]
+    peers += [at(x, y, z, 1 - core)]
+    greet(peers)
+
+    def columns(color):
+        return dp_ref.at[:, pl.ds(color * half, half)]
+
+    def lanes(slot):
+        return xg.at[:, :, pl.ds(pl.multiple_of(slot * t, t), t)]
+
+    def x_line(j):
+        k, slot = (x + j) % NX, x * 2 + core
+        peer = at(k, y, z, 0)
+        return (send(xt_ref.at[k], lanes(slot), x_send.at[0, j], x_recv.at[slot], peer),
+                send(columns(0), pg.at[slot], p_send.at[0, j], p_recv.at[slot], peer))
+
+    def y_line(j):
+        k, slot = (y + j) % NY, y * 2 + core
+        peer = at(x, k, z, 1)
+        return (send(xt_ref.at[:, k], lanes(slot), x_send.at[1, j], x_recv.at[slot], peer),
+                send(columns(1), pg.at[slot], p_send.at[1, j], p_recv.at[slot], peer))
+
+    for j in (2, 1, 3):
+        for copy in x_line(j) + y_line(j):
+            copy.start()
+
+    @pl.when(core == 0)
+    def _():
+        for copy in y_line(0):
+            copy.start()
+        pltpu.make_async_copy(xt_ref.at[x], lanes(x * 2), x_recv.at[x * 2]).start()
+        pltpu.make_async_copy(columns(0), pg.at[x * 2], p_recv.at[x * 2]).start()
+
+    @pl.when(core == 1)
+    def _():
+        for copy in x_line(0):
+            copy.start()
+        pltpu.make_async_copy(xt_ref.at[:, y], lanes(y * 2 + 1), x_recv.at[y * 2 + 1]).start()
+        pltpu.make_async_copy(columns(1), pg.at[y * 2 + 1], p_recv.at[y * 2 + 1]).start()
+
+    def emb_copy(j):
+        return send(rows.at[j], emb_ref.at[z], e_send.at[j], e_recv.at[j], at(x, y, (z + 1 + j) % NZ, core))
+
+    emb_home = pltpu.make_async_copy(rows.at[NZ - 1], emb_ref.at[z], e_send.at[NZ - 1])
+    for j in range(NZ):
+        pltpu.make_async_copy(w_ref.at[pl.ds(0, width)], wv.at[j], w_sem.at[j]).wait()
+        rows[j] = lax.dot_general(
+            dp_ref[...], wv[j], (((1,), (1,)), ((), ())), preferred_element_type=jnp.float32
+        ).astype(jnp.bfloat16)
+        if j < NZ - 1:
+            emb_copy(j).start()
+        else:
+            emb_home.start()
+
+    for slot in range(8):
+        pltpu.make_async_copy(xt_ref.at[0], lanes(slot), x_recv.at[slot]).wait()
+        pltpu.make_async_copy(columns(0), pg.at[slot], p_recv.at[slot]).wait()
+
+    p = (1 - core) * y + core * x
+
+    def second(j):
+        k = (p + 1 + j) % NX
+        peer = at((1 - core) * x + core * k, (1 - core) * k + core * y, z, core)
+        return send(s2.at[j], r2.at[j], send2.at[j], recv2.at[j], peer)
+
+    right = pg[...].reshape(8 * t, half)
+    for j in range(NX):
+        k = (p + 1 + j) % NX
+        part = jnp.dot(xg[k], right, preferred_element_type=jnp.float32)
+        if j < NX - 1:
+            s2[j] = part.astype(jnp.bfloat16)
+            second(j).start()
+        else:
+            own[...] = part
+    for j in range(NX - 1):
+        second(j).wait_recv()
+    total = own[...] + r2[0].astype(jnp.float32) + r2[1].astype(jnp.float32) + r2[2].astype(jnp.float32)
+    total = (total * scale).astype(jnp.float32)
+    own[...] = total
+    me = z * 2 + core
+    for slot in range(2 * NZ):
+        s3[slot] = own[8 * slot:8 * slot + 8].astype(jnp.bfloat16)
+
+    def third(j):
+        slot = (me + j) % (2 * NZ)
+        return send(s3.at[slot], r3.at[me], send3.at[j], recv3.at[me], at(x, y, slot // 2, slot % 2))
+
+    for j in range(1, 2 * NZ):
+        third(j).start()
+    r3[me] = s3[me]
+    for j in range(1, 2 * NZ):
+        slot = (me + j) % (2 * NZ)
+        send(s3.at[0], r3.at[slot], send3.at[j], recv3.at[slot], at(x, y, slot // 2, slot % 2)).wait_recv()
+    for color in range(2):
+        acc = r3[color].astype(jnp.float32)
+        for c in range(1, NZ):
+            acc = acc + r3[2 * c + color].astype(jnp.float32)
+        dw_ref[:, color * half:(color + 1) * half] = acc
+
+    for j in range(1, NX):
+        for copy in x_line(j) + y_line(j):
+            copy.wait_send()
+
+    @pl.when(core == 0)
+    def _():
+        for copy in y_line(0):
+            copy.wait_send()
+
+    @pl.when(core == 1)
+    def _():
+        for copy in x_line(0):
+            copy.wait_send()
+
+    for j in range(NX - 1):
+        second(j).wait_send()
+    for j in range(1, 2 * NZ):
+        third(j).wait_send()
+    for j in range(NZ - 1):
+        emb_copy(j).wait_send()
+    for j in range(NZ - 1):
+        emb_copy(j).wait_recv()
+    emb_home.wait()
+
+
+def grads(d_proj, x_rows, w_in, scale):
+    t, e = d_proj.shape
+    d = x_rows.shape[1]
+    half, width, part = e // 2, d // NZ, d // NX // NY
+    xt = x_rows.T.reshape(NZ, NX, NY, part // NZ, t).transpose(1, 2, 0, 3, 4).reshape(NX, NY, part, t)
+    dma = pltpu.SemaphoreType.DMA
+    vmem = pl.BlockSpec(memory_space=pltpu.VMEM)
+    hbm = pl.BlockSpec(memory_space=pl.ANY)
+    return pl.pallas_call(
+        functools.partial(grad_kernel, scale),
+        name="grads",
+        out_shape=(jax.ShapeDtypeStruct((NZ, t, width), jnp.bfloat16),
+                   jax.ShapeDtypeStruct((part // NZ // 2, e), jnp.float32)),
+        in_specs=[vmem, vmem, hbm],
+        out_specs=(hbm, vmem),
+        scratch_shapes=[
+            pltpu.VMEM((NZ, width, e), jnp.bfloat16),
+            pltpu.VMEM((NX, part, 8 * t), jnp.bfloat16),
+            pltpu.VMEM((8, t, half), jnp.bfloat16),
+            pltpu.VMEM((NZ, t, width), jnp.bfloat16),
+            pltpu.VMEM((NX - 1, part, half), jnp.bfloat16),
+            pltpu.VMEM((NX - 1, part, half), jnp.bfloat16),
+            pltpu.VMEM((2 * NZ, part // NZ // 2, half), jnp.bfloat16),
+            pltpu.VMEM((2 * NZ, part // NZ // 2, half), jnp.bfloat16),
+            pltpu.VMEM((part, half), jnp.float32),
+            dma((NZ,)), dma((2, NX)), dma((8,)), dma((2, NX)), dma((8,)), dma((NZ,)), dma((NZ,)),
+            dma((NX,)), dma((NX,)), dma((2 * NZ,)), dma((2 * NZ,)),
+        ],
+        compiler_params=pltpu.CompilerParams(collective_id=0, has_side_effects=True, vmem_limit_bytes=60 * 1024 * 1024),
+    )(d_proj, xt, w_in)
+
+
 def on_device(embeds, w_in, log_decay, clip_keep, clip_starts, valid_len, norm_gain, g_out):
     n_cam = lax.axis_size("cam")
     n_tm = lax.axis_size("tm")
@@ -113,17 +311,8 @@
     d_proj = jnp.concatenate(
         [du_rows, d_b.reshape(t_dev, N), d_c.reshape(t_dev, N)], axis=1
     ).astype(jnp.bfloat16)
-    all_proj = lax.all_gather(d_proj, "cam").reshape(n_cam * t_dev, HP + 2 * N)
-    width = D // n_cam
-    w_mine = lax.dynamic_slice_in_dim(w_in, lax.axis_index("cam") * width, width, axis=0)
-    d_embeds = lax.dot_general(
-        all_proj, w_mine, (((1,), (1,)), ((), ())), preferred_element_type=jnp.float32
-    ).astype(jnp.bfloat16).reshape(n_cam, t_dev, width)
     grad_scale = 1.0 / math.sqrt(n_cam * t_dev * n_tm)
-    row_terms = grad_scale * lax.dot_general(
-        embeds.reshape(n_cam * t_dev, width), all_proj, (((0,), (0,)), ((), ())), preferred_element_type=jnp.float32
-    )
-    d_w_in = lax.psum_scatter(row_terms, "tm", scatter_dimension=0, tiled=True)
+    d_embeds, d_w_in = grads(d_proj, x_rows, w_in, grad_scale)
     return (layer_out[None], d_embeds, d_w_in)
 
 

time: 302 us -> 198 us (0.66)
  waiting for transfers between devices: 181 us -> 45 us
  Pallas kernels: 0 us -> 45.3 us
  between operations: 15.1 us -> 1.69 us
  matrix products: 46 us -> 36 us
  local copies, waits for them, and re-layouts: 17 us -> 25.5 us
    unnamed x3 -> x0, waiting for transfers between devices: 77.7 us -> none
    all_gather x1 -> x0, waiting for transfers between devices: 51.8 us -> none  [on_device(): all_proj = lax.all_gather(d_proj, 'cam').reshape(n_cam * t_dev, HP + 2 * N)]
    pallas_call x0 -> x1, Pallas kernels: none -> 45.3 us  [grads(): pl.pallas_call(functools.partial(grad_kernel, scale), name='grads', out_s...]
    all_to_all x2, waiting for transfers between devices: 30.3 us -> 18.1 us  [prefix_states(): mine = lax.all_to_all(packed, 'tm', split_axis=0, concat_axis=0, tiled=True)]
    dot_general x2 -> x0, matrix products: 8.79 us -> none  [the longest x1 4.9 us: on_device(): lax.dot_general(all_proj, w_mine, (((1,), (1,)), ((), ())), preferred_ele...]
    all_to_all x2, waiting for transfers between devices: 5.48 us -> 10.7 us  [prefix_states(): lax.all_to_all(entered, 'tm', split_axis=0, concat_axis=0, tiled=True)]
    mul x2, local copies, waits for them, and re-layouts: 0.4 us -> 3.72 us  [on_device(): normed = raw_out * inv_rms]
    unnamed x18 -> x31, local copies, waits for them, and re-layouts: 5.9 us -> 9.08 us
  transfers between devices with their start and end apart: 7 -> 5, of which waited for: 7 -> 4; matrix products, arithmetic and copies ran while one was open for 11% -> 16% of each run, Pallas kernels for 0% -> 0%
where the time goes in v2:
time: 198 us; the launch traced here: 197 us
  Pallas kernels  45.3 us (23%)
  waiting for transfers between devices  45 us (23%)
  matrix products  36 us (18%)
  starting transfers between devices  34 us (17%)
  local copies, waits for them, and re-layouts  25.5 us (13%)
  other arithmetic  9.44 us (5%)
    pallas_call x1, Pallas kernels, grads(): pl.pallas_call(functools.partial(grad_kernel, scale), name='grads', out_s...  45.3 us
    all_to_all x2, waiting for transfers between devices, prefix_states(): mine = lax.all_to_all(packed, 'tm', split_axis=0, concat_axis=0, tiled=True)  18.1 us
    all_to_all x1, waiting for transfers between devices, on_device(): lax.all_to_all(embeds, 'cam', split_axis=0, concat_axis=2, tiled=True)[0]  16.1 us
    all_to_all x2, starting transfers between devices, prefix_states(): mine = lax.all_to_all(packed, 'tm', split_axis=0, concat_axis=0, tiled=True)  13.8 us
    all_to_all x2, starting transfers between devices, prefix_states(): lax.all_to_all(entered, 'tm', split_axis=0, concat_axis=0, tiled=True)  11.2 us
    all_to_all x2, waiting for transfers between devices, prefix_states(): lax.all_to_all(entered, 'tm', split_axis=0, concat_axis=0, tiled=True)  10.7 us
    unnamed x31, local copies, waits for them, and re-layouts  9.08 us
    all_to_all x1, starting transfers between devices, on_device(): lax.all_to_all(embeds, 'cam', split_axis=0, concat_axis=2, tiled=True)[0]  9 us
  transfers between devices with their start and end apart: 5, of which 4 were waited for; matrix products, arithmetic and copies ran while one was open for 16% of the time, Pallas kernels for 0%

profile of v2, /device:TPU:1, one launch (start us, length us, event | category | flops | bytes accessed | tf_op | source)
XLA Modules:
  0.0 196.9 jit_solution(12983145862245463124)
XLA Ops:
  0.7 2.1 %copy.42 = bf16[8,128,256]{1,2,0:T(8,128)(2,1)} copy(bf16[8,128,256]{2,1,0:T(8,128)(2,1)} %param.8) | data formatting | bytes 1048576 | tf_op args[0]
  2.7 9.0 %all-to-all-start = ((bf16[8,128,256]{1,2,0:T(8,128)(2,1)}), bf16[8,128,256]{1,2,0:T(8,128)(2,1)S(1)}, u32[]{:S(2)}, u32[]{:S(2)}) async-start(bf16[8,128,256]{1,2,0:T(8,128)(2,1)} %copy.42), calls=%async_computation | async-start | bytes 1048576 | tf_op jit(solution)/shard_map/all_to_all | solution.py:244
  13.6 16.1 %all-to-all-done = bf16[8,128,256]{1,2,0:T(8,128)(2,1)S(1)} async-done(((bf16[8,128,256]{1,2,0:T(8,128)(2,1)}), bf16[8,128,256]{1,2,0:T(8,128)(2,1)S(1)}, u32[]{:S(2)}, u32[]{:S(2)}) %all-to-all-start) | async-done | bytes 524320 | tf_op jit(solution)/shard_map/all_to_all | solution.py:244
  29.7 5.3 %convolution_convert_fusion.2 = bf16[128,2304]{1,0:T(8,128)(2,1)S(1)} fusion(bf16[128,2048]{0,1:T(8,128)(2,1)S(1)} %bitcast.115, bf16[2048,2304]{1,0:T(8,128)(2,1)} %w_ref.1), kind=kOutput, calls=%fused_computation.2 | convolution fusion | flops 1208254464 | bytes 10551296 | tf_op jit(solution)/shard_map/dot_general | solution.py:245
  36.2 1.5 copy.45
  39.6 7.6 %all-to-all-start.1 = ((f32[32,72,128]{2,1,0:T(8,128)}), f32[32,72,128]{2,1,0:T(8,128)}, u32[]{:S(2)}, u32[]{:S(2)}) async-start(f32[32,72,128]{2,1,0:T(8,128)} %pad_maximum_fusion.1), calls=%async_computation.1 | async-start | bytes 2359296 | tf_op jit(solution)/shard_map/all_to_all | solution.py:29
  47.6 18.1 %all-to-all-done.1 = f32[32,72,128]{2,1,0:T(8,128)} async-done(((f32[32,72,128]{2,1,0:T(8,128)}), f32[32,72,128]{2,1,0:T(8,128)}, u32[]{:S(2)}, u32[]{:S(2)}) %all-to-all-start.1) | async-done | bytes 1179680 | tf_op jit(solution)/shard_map/all_to_all | solution.py:29
  65.7 1.2 slice_reduce_fusion.2
  67.1 1.3 slice.41
  68.4 1.6 fusion.15
  70.9 3.9 %all-to-all-start.2 = ((bf16[32,64,128]{2,1,0:T(8,128)(2,1)}), bf16[32,64,128]{2,1,0:T(8,128)(2,1)S(1)}, u32[]{:S(2)}, u32[]{:S(2)}) async-start(bf16[32,64,128]{2,1,0:T(8,128)(2,1)} %bitcast.123), calls=%async_computation.2 | async-start | bytes 1048576 | tf_op jit(solution)/shard_map/all_to_all | solution.py:43
  75.9 2.5 %copy.43 = f32[128,2048]{0,1:T(8,128)} copy(f32[128,2048]{1,0:T(8,128)} %slice_convert_fusion) | data formatting | bytes 2097152 | tf_op jit(solution)/shard_map/slice | solution.py:251
  78.6 6.5 %fusion.5 = f32[1,128,32,64]{1,3,2,0:T(8,128)} fusion(f32[128,128]{1,0:T(8,128)S(1)} %fusion.59, f32[32,128]{1,0:T(8,128)S(1)} %bitcast.127, pred[128,128]{1,0:T(8,128)(4,1)S(1)} %iota_compare_fusion, f32[128,32,64]{0,2,1:T(8,128)} %bitcast.124, f32[128]{0:T(128)S(1)} %compare_convert_fusion), kind=kOutput, calls=%fused_computation.10 | convolution fusion | flops 405012480 | bytes 2195968 | tf_op jit(solution)/shard_map/khts,kshp->kthp/dot_general | solution.py:263
  85.1 1.3 all-to-all-done.2
  87.2 2.2 %fusion.27 = (f32[128,32]{0,1:T(8,128)S(1)}, f32[1,128,32,64]{1,3,2,0:T(8,128)S(1)}) fusion(f32[1,128,32,64]{1,3,2,0:T(8,128)} %fusion.5, bf16[32,64,128]{2,1,0:T(8,128)(2,1)} %copy-done.5, f32[32]{0:T(128)S(1)} %get-tuple-element.13, bf16[128,2304]{1,0:T(8,128)(2,1)} %copy-done.4, f32[128,32]{0,1:T(8,128)S(1)} %get-tuple-element.11), kind=kOutput, calls=%fused_computation.38 | convolution fusion | flops 404221952 | bytes 2687104 | tf_op jit(solution)/shard_map/khpn,ktn->kthp/dot_general | solution.py:275
  91.2 1.4 convolution_add_fusion
  93.7 6.1 %all-to-all-start.3 = ((f32[32,72,128]{2,1,0:T(8,128)}), f32[32,72,128]{2,1,0:T(8,128)}, u32[]{:S(2)}, u32[]{:S(2)}) async-start(f32[32,72,128]{2,1,0:T(8,128)} %pad_maximum_fusion), calls=%async_computation.3 | async-start | bytes 2359296 | tf_op jit(solution)/shard_map/all_to_all | solution.py:29
  101.8 2.6 %copy.48 = f32[1,128,2048]{2,1,0:T(8,128)} copy(f32[1,128,2048]{1,2,0:T(8,128)} %bitcast.120) | data formatting | bytes 2097152 | tf_op jit(solution)/shard_map/mul | solution.py:280
  104.4 1.3 copy.47
  105.8 3.0 %convolution_bitcast_fusion = f32[128,128]{1,0:T(8,128)S(1)} fusion(bf16[32,64,128]{2,1,0:T(8,128)(2,1)} %copy-done.5, f32[1,128,32,64]{1,3,2,0:T(8,128)S(1)} %copy-done.1, f32[128,32]{0,1:T(8,128)S(1)} %get-tuple-element.11, f32[32]{0:T(128)S(1)} %get-tuple-element.13), kind=kOutput, calls=%fused_computation.22 | convolution fusion | flops 403439616 | bytes 1654912 | tf_op jit(solution)/shard_map/kthp,khpn->ktn/dot_general | solution.py:303
  108.7 5.2 %multiply_reduce_fusion = f32[128,128]{1,0:T(8,128)S(1)} fusion(f32[1,128,32,64]{1,3,2,0:T(8,128)S(1)} %copy-done.1, f32[32,128]{1,0:T(8,128)S(1)} %bitcast.128, pred[128,128]{1,0:T(8,128)(4,1)S(1)} %iota_compare_fusion, f32[128,32,64]{0,2,1:T(8,128)} %bitcast.125, f32[128]{0:T(128)S(1)} %compare_convert_fusion), kind=kOutput, calls=%fused_computation.3 | convolution fusion | flops 405520384 | bytes 2195968 | tf_op jit(solution)/shard_map/kthp,kshp->khts/dot_general | solution.py:301
  114.9 3.4 %fusion.8 = f32[1,128,32,64]{1,3,2,0:T(8,128)} fusion(f32[1,128,32,64]{1,3,2,0:T(8,128)S(1)} %copy-done.1, f32[128,128]{1,0:T(8,128)S(1)} %fusion.59, f32[32,128]{1,0:T(8,128)S(1)} %bitcast.129, pred[128,128]{1,0:T(8,128)(4,1)S(1)} %iota_compare_fusion), kind=kOutput, calls=%fused_computation.11 | convolution fusion | flops 404750336 | bytes 2195456 | tf_op jit(solution)/shard_map/khts,kthp->kshp/dot_general | solution.py:297
  119.7 1.3 slice.43
  121.0 1.6 fusion.16
  123.5 7.4 %all-to-all-start.4 = ((bf16[32,64,128]{2,1,0:T(8,128)(2,1)}), bf16[32,64,128]{2,1,0:T(8,128)(2,1)S(1)}, u32[]{:S(2)}, u32[]{:S(2)}) async-start(bf16[32,64,128]{2,1,0:T(8,128)(2,1)} %bitcast.55), calls=%async_computation.4 | async-start | bytes 1048576 | tf_op jit(solution)/shard_map/all_to_all | solution.py:43
  130.9 2.2 %multiply_convert_fusion.1 = bf16[1,128,2048]{2,1,0:T(8,128)(2,1)} fusion(f32[1,128,2048]{2,1,0:T(8,128)} %copy.47, f32[1,128,2048]{2,1,0:T(8,128)S(1)} %copy-done.6, f32[128]{0:T(128)S(1)} %compare_convert_fusion, f32[2048]{0:T(1024)S(1)} %copy-done.9), kind=kLoop, calls=%fused_computation.44 | loop fusion | flops 1048576 | bytes 2630144 | tf_op jit(solution)/shard_map/convert_element_type | solution.py:281
  133.1 9.4 %all-to-all-done.4 = bf16[32,64,128]{2,1,0:T(8,128)(2,1)S(1)} async-done(((bf16[32,64,128]{2,1,0:T(8,128)(2,1)}), bf16[32,64,128]{2,1,0:T(8,128)(2,1)S(1)}, u32[]{:S(2)}, u32[]{:S(2)}) %all-to-all-start.4) | async-done | bytes 524320 | tf_op jit(solution)/shard_map/all_to_all | solution.py:43
  142.5 1.9 convolution_bitcast_fusion.1
  145.4 1.5 fusion.14
  148.2 45.3 %grads.1 = (bf16[8,128,256]{2,1,0:T(8,128)(2,1)}, f32[8,2304]{1,0:T(8,128)}) custom-call(bf16[128,2304]{1,0:T(8,128)(2,1)} %pad_maximum_fusion.2.dp_ref, bf16[4,4,128,128]{3,2,1,0:T(8,128)(2,1)} %bitcast.122, bf16[2048,2304]{1,0:T(8,128)(2,1)} %w_ref.1), custom_call_target="tpu_custom_call" | custom-call | tf_op jit(solution)/shard_map/grads/pallas_call | solution.py:215
  193.5 1.9 copy.79
  195.4 1.5 copy.80
  (68 shorter events, 18.1 us)
Async XLA Ops:
  0.6 11.1 %copy-start.11 = (s32[1,3]{1,0:T(1,128)S(1)}, s32[1,3]{1,0:T(1,128)}, u32[]{:S(2)}) copy-start(s32[1,3]{1,0:T(1,128)} %param.12) | copy-start | bytes 40
  0.6 11.8 %copy-start.12 = (f32[32]{0:T(128)S(1)}, f32[32]{0:T(128)}, u32[]{:S(2)}) copy-start(f32[32]{0:T(128)} %param.11) | copy-start | bytes 388
  0.7 11.9 %copy-start.10 = (f32[1,32,128]{2,1,0:T(8,128)S(1)}, f32[1,32,128]{2,1,0:T(8,128)}, u32[]{:S(2)}) copy-start(f32[1,32,128]{2,1,0:T(8,128)} %param.10) | copy-start | bytes 49156
  2.7 27.0 %all-to-all-start = ((bf16[8,128,256]{1,2,0:T(8,128)(2,1)}), bf16[8,128,256]{1,2,0:T(8,128)(2,1)S(1)}, u32[]{:S(2)}, u32[]{:S(2)}) async-start(bf16[8,128,256]{1,2,0:T(8,128)(2,1)} %copy.42), calls=%async_computation | async-start | bytes 1048576 | tf_op jit(solution)/shard_map/all_to_all | solution.py:244
  29.7 5.3 %copy-start.2 = (bf16[8,128,256]{1,2,0:T(8,128)(2,1)}, bf16[8,128,256]{1,2,0:T(8,128)(2,1)S(1)}, u32[]{:S(2)}) copy-start(bf16[8,128,256]{1,2,0:T(8,128)(2,1)S(1)} %all-to-all-done) | copy-start | bytes 1572868
  35.0 43.4 %copy-start.4 = (bf16[128,2304]{1,0:T(8,128)(2,1)}, bf16[128,2304]{1,0:T(8,128)(2,1)S(1)}, u32[]{:S(2)}) copy-start(bf16[128,2304]{1,0:T(8,128)(2,1)S(1)} %convolution_convert_fusion.2) | copy-start | bytes 1769476
  38.4 8.8 %copy-start.9 = (f32[2048]{0:T(1024)S(1)}, f32[2048]{0:T(1024)}, u32[]{:S(2)}) copy-start(f32[2048]{0:T(1024)} %param.14) | copy-start | bytes 24580
  38.5 8.9 %copy-start.8 = (bf16[1,128,2048]{2,1,0:T(8,128)(2,1)S(1)}, bf16[1,128,2048]{2,1,0:T(8,128)(2,1)}, u32[]{:S(2)}) copy-start(bf16[1,128,2048]{2,1,0:T(8,128)(2,1)} %param.15) | copy-start | bytes 1572868
  39.6 26.1 %all-to-all-start.1 = ((f32[32,72,128]{2,1,0:T(8,128)}), f32[32,72,128]{2,1,0:T(8,128)}, u32[]{:S(2)}, u32[]{:S(2)}) async-start(f32[32,72,128]{2,1,0:T(8,128)} %pad_maximum_fusion.1), calls=%async_computation.1 | async-start | bytes 2359296 | tf_op jit(solution)/shard_map/all_to_all | solution.py:29
  70.9 15.5 %all-to-all-start.2 = ((bf16[32,64,128]{2,1,0:T(8,128)(2,1)}), bf16[32,64,128]{2,1,0:T(8,128)(2,1)S(1)}, u32[]{:S(2)}, u32[]{:S(2)}) async-start(bf16[32,64,128]{2,1,0:T(8,128)(2,1)} %bitcast.123), calls=%async_computation.2 | async-start | bytes 1048576 | tf_op jit(solution)/shard_map/all_to_all | solution.py:43
  86.4 0.8 copy-start.5
  90.2 1.0 copy-start
  92.6 7.3 %copy-start.3 = (bf16[8,128,256]{1,2,0:T(8,128)(2,1)S(1)}, bf16[8,128,256]{1,2,0:T(8,128)(2,1)}, u32[]{:S(2)}) copy-start(bf16[8,128,256]{1,2,0:T(8,128)(2,1)} %copy-done.2) | copy-start | bytes 1572868
  93.7 24.5 %all-to-all-start.3 = ((f32[32,72,128]{2,1,0:T(8,128)}), f32[32,72,128]{2,1,0:T(8,128)}, u32[]{:S(2)}, u32[]{:S(2)}) async-start(f32[32,72,128]{2,1,0:T(8,128)} %pad_maximum_fusion), calls=%async_computation.3 | async-start | bytes 2359296 | tf_op jit(solution)/shard_map/all_to_all | solution.py:29
  101.8 4.0 %copy-start.1 = (f32[1,128,32,64]{1,3,2,0:T(8,128)S(1)}, f32[1,128,32,64]{1,3,2,0:T(8,128)}, u32[]{:S(2)}) copy-start(f32[1,128,32,64]{1,3,2,0:T(8,128)} %copy-done) | copy-start | bytes 3145732
  121.0 9.9 %copy-start.6 = (f32[1,128,2048]{2,1,0:T(8,128)S(1)}, f32[1,128,2048]{2,1,0:T(8,128)}, u32[]{:S(2)}) copy-start(f32[1,128,2048]{2,1,0:T(8,128)} %copy.48) | copy-start | bytes 3145732
  123.5 19.0 %all-to-all-start.4 = ((bf16[32,64,128]{2,1,0:T(8,128)(2,1)}), bf16[32,64,128]{2,1,0:T(8,128)(2,1)S(1)}, u32[]{:S(2)}, u32[]{:S(2)}) async-start(bf16[32,64,128]{2,1,0:T(8,128)(2,1)} %bitcast.55), calls=%async_computation.4 | async-start | bytes 1048576 | tf_op jit(solution)/shard_map/all_to_all | solution.py:43
  133.1 12.3 %copy-start.7 = (f32[1,128,32,64]{1,3,2,0:T(8,128)S(1)}, f32[1,128,32,64]{1,3,2,0:T(8,128)}, u32[]{:S(2)}) copy-start(f32[1,128,32,64]{1,3,2,0:T(8,128)} %fusion.8) | copy-start | bytes 3145732

commit v3 on v2

--- a/solution.py
+++ b/solution.py
@@ -17,30 +17,8 @@
 
 
 epsilon = 1e-05
-precise = lax.Precision.HIGHEST
 MESH = pl.DeviceIdType.MESH
 NX, NY, NZ = 4, 4, 8
-
-
-def prefix_states(block_log, state, reverse):
-    size = lax.axis_size("tm")
-    extra = jnp.broadcast_to(block_log[:, None, None], (H, 8, N))
-    packed = jnp.concatenate([state, extra], axis=1)
-    mine = lax.all_to_all(packed, "tm", split_axis=0, concat_axis=0, tiled=True)
-    logs = mine[:, P_SIZE, 0]
-    parts = mine[:, :P_SIZE].reshape(size, P_SIZE * N)
-    cum = jnp.cumsum(logs)
-    at = jnp.arange(size)
-    if reverse:
-        reach = at[None, :] > at[:, None]
-        gap = (cum - logs)[None, :] - cum[:, None]
-    else:
-        reach = at[None, :] < at[:, None]
-        gap = (cum - logs)[:, None] - cum[None, :]
-    factors = jnp.where(reach, jnp.exp(jnp.where(reach, gap, 0.0)), 0.0)
-    entered = jnp.dot(factors, parts, precision=precise).astype(jnp.bfloat16)
-    entered = entered.reshape(size, P_SIZE, N)
-    return lax.all_to_all(entered, "tm", split_axis=0, concat_axis=0, tiled=True).astype(jnp.float32)
 
 
 def place():
@@ -236,81 +214,214 @@
     )(d_proj, xt, w_in)
 
 
+def scan_kernel(lg_ref, w_ref, cum_ref, valid_ref, proj_ref, xt_ref, gt_ref, gain_ref, out_ref, dp_ref,
+                tail, lift, xw, mix, yin, dt, dl, din, lot, lgot, snd1, got1, snd2, sin, snd3, got3, snd4, rin,
+                l_send, l_recv, send1, recv1, send2, recv2, send3, recv3, send4, recv4):
+    heads = H
+    f32, b16 = jnp.float32, jnp.bfloat16
+    me, cam = lax.axis_index("tm"), lax.axis_index("cam")
+    n_tm = 2 * NX * NY
+    hp = heads * P_SIZE
+    barrier = pltpu.get_barrier_semaphore()
+
+    def greet_one(j, _):
+        pl.semaphore_signal(barrier, inc=1, device_id=(cam, (me + j) % n_tm), device_id_type=MESH)
+        return 0
+
+    lax.fori_loop(1, n_tm, greet_one, 0)
+    pl.semaphore_wait(barrier, n_tm - 1)
+
+    def exchange(src, dst, sem_a, sem_b):
+        def copy(j):
+            peer = (me + j) % n_tm
+            return send(src.at[peer], dst.at[me], sem_a.at[j], sem_b.at[j], (cam, peer))
+
+        def start():
+            def body(j, _):
+                copy(j).start()
+                return 0
+            lax.fori_loop(1, n_tm, body, 0)
+            dst[me] = src[me]
+
+        def arrive():
+            def body(j, _):
+                copy(j).wait_recv()
+                return 0
+            lax.fori_loop(1, n_tm, body, 0)
+
+        def sent():
+            def body(j, _):
+                copy(j).wait_send()
+                return 0
+            lax.fori_loop(1, n_tm, body, 0)
+        return start, arrive, sent
+
+    logs = exchange(lg_ref, lgot, l_send, l_recv)
+    fwd_out = exchange(snd1, got1, send1, recv1)
+    fwd_back = exchange(snd2, sin, send2, recv2)
+    bwd_out = exchange(snd3, got3, send3, recv3)
+    bwd_back = exchange(snd4, rin, send4, recv4)
+    logs[0]()
+
+    b_nat, c_nat = proj_ref[:, hp:hp + N], proj_ref[:, hp + N:hp + 2 * N]
+    b_t, c_t = xt_ref[hp:hp + N], xt_ref[hp + N:hp + 2 * N]
+    cum = cum_ref[...]
+    tail[...] = jnp.exp(cum[:, Q - 1:Q] - cum)
+    lift[...] = jnp.exp(cum)
+    valid = valid_ref[0:1]
+    group = 4
+    steps = heads // group
+
+    def dot(a, b):
+        return jnp.dot(a, b, preferred_element_type=f32)
+
+    def dot_t(a, b):
+        return lax.dot_general(a, b, (((1,), (1,)), ((), ())), preferred_element_type=f32)
+
+    def t_dot(a, b):
+        return lax.dot_general(a, b, (((0,), (0,)), ((), ())), preferred_element_type=f32)
+
+    def each(body, init=0):
+        return lax.fori_loop(0, steps, body, init)
+
+    def rows(g, i):
+        return pl.ds(pl.multiple_of((g * group + i) * P_SIZE, P_SIZE), P_SIZE)
+
+    def local_states(g, _):
+        for i in range(group):
+            h = g * group + i
+            xw[h] = (xt_ref[rows(g, i)].astype(f32) * tail[pl.ds(h, 1)]).astype(b16)
+        states = dot(xw[pl.ds(g * group, group)].reshape(group * P_SIZE, Q), b_nat)
+        snd1[pl.ds(g * group, group)] = states.astype(b16).reshape(group, P_SIZE, N)
+        return 0
+
+    each(local_states)
+    fwd_out[0]()
+
+    scores = dot(b_nat, c_t)
+
+    def inside(g, _):
+        for i in range(group):
+            h = g * group + i
+            mix[h] = (w_ref[h] * scores).astype(b16)
+            yin[h] = dot(xt_ref[rows(g, i)], mix[h])
+        return 0
+
+    each(inside)
+    logs[1]()
+    fwd_out[1]()
+
+    def scan(parts, out, reverse):
+        def body(k, state):
+            i = n_tm - 1 - k if reverse else k
+            out[i] = state.astype(b16).reshape(P_SIZE, N)
+            decay = jnp.exp(lgot[i])
+            return decay[None] * state + parts[i].astype(f32).reshape(P_SIZE // 8, 8, N)
+        lax.fori_loop(0, n_tm, body, jnp.zeros((P_SIZE // 8, 8, N), f32))
+
+    scan(got1, snd2, False)
+    fwd_back[0]()
+    fwd_back[1]()
+
+    def norm_step(g, _):
+        carried = dot(sin[pl.ds(g * group, group)].reshape(group * P_SIZE, N), c_t)
+        for i in range(group):
+            h = g * group + i
+            up = lift[pl.ds(h, 1)]
+            raw = yin[h] + up * carried[i * P_SIZE:(i + 1) * P_SIZE]
+            inv = lax.rsqrt(jnp.mean(raw * raw, axis=0, keepdims=True) + epsilon)
+            normed = raw * inv
+            gain = gain_ref[rows(g, i)] * valid
+            lot[rows(g, i)] = normed * gain
+            d_normed = gt_ref[rows(g, i)].astype(f32) * gain
+            d_out = inv * (d_normed - normed * jnp.mean(d_normed * normed, axis=0, keepdims=True))
+            dt[h] = d_out.astype(b16)
+            dl[h] = (d_out * up).astype(b16)
+        states = dot(dl[pl.ds(g * group, group)].reshape(group * P_SIZE, Q), c_nat)
+        snd3[pl.ds(g * group, group)] = states.astype(b16).reshape(group, P_SIZE, N)
+        return 0
+
+    each(norm_step)
+    bwd_out[0]()
+
+    first = lax.broadcasted_iota(jnp.int32, (2 * P_SIZE, Q), 0) < P_SIZE
+
+    def pairs(g, total):
+        for i in range(0, group, 2):
+            h = g * group + i
+            d_two = dt[pl.ds(h, 2)].reshape(2 * P_SIZE, Q)
+            zero = jnp.zeros_like(d_two)
+            spread = jnp.concatenate([jnp.where(first, d_two, zero), jnp.where(first, zero, d_two)], axis=1)
+            x_two = proj_ref[:, pl.ds(pl.multiple_of(h * P_SIZE, 2 * P_SIZE), 2 * P_SIZE)]
+            both = dot(x_two, spread)
+            total = total + w_ref[h] * both[:, :Q] + w_ref[h + 1] * both[:, Q:]
+            din[h] = dot_t(dt[h], mix[h])
+            din[h + 1] = dot_t(dt[h + 1], mix[h + 1])
+        return total
+
+    pair_sum = each(pairs, jnp.zeros((Q, Q), f32)).astype(b16)
+    d_c = t_dot(pair_sum, b_nat) + t_dot(dl[...].reshape(hp, Q), sin[...].reshape(hp, N))
+    d_b = dot(pair_sum, c_nat)
+    dp_ref[:, hp + N:hp + 2 * N] = d_c.astype(b16)
+    for k in range(hp // Q):
+        out_ref[:, k * Q:(k + 1) * Q] = lot[k * Q:(k + 1) * Q].T.astype(b16)
+    bwd_out[1]()
+    scan(got3, snd4, True)
+    bwd_back[0]()
+    bwd_back[1]()
+    d_b = d_b + t_dot(xw[...].reshape(hp, Q), rin[...].reshape(hp, N))
+    dp_ref[:, hp:hp + N] = d_b.astype(b16)
+    for k in range(heads // 2):
+        after = dot(rin[2 * k:2 * k + 2].reshape(2 * P_SIZE, N), b_t)
+        two = [din[2 * k + i] + tail[2 * k + i:2 * k + i + 1] * after[i * P_SIZE:(i + 1) * P_SIZE] for i in range(2)]
+        dp_ref[:, k * Q:(k + 1) * Q] = (jnp.concatenate(two, axis=0) * valid).T.astype(b16)
+    for _, _, sent in (logs, fwd_out, fwd_back, bwd_out, bwd_back):
+        sent()
+
+
+def scan_both(lg, weights, cum, valid, proj, proj_t, g_t, gain):
+    n_tm = lg.shape[0]
+    hp = H * P_SIZE
+    dma = pltpu.SemaphoreType.DMA
+    vmem = pl.BlockSpec(memory_space=pltpu.VMEM)
+    f32, b16 = jnp.float32, jnp.bfloat16
+    states = pltpu.VMEM((n_tm, P_SIZE, N), b16)
+    return pl.pallas_call(
+        scan_kernel,
+        name="scan_both",
+        out_shape=(jax.ShapeDtypeStruct((Q, hp), b16), jax.ShapeDtypeStruct((Q, hp + 2 * N), b16)),
+        in_specs=[vmem] * 8,
+        out_specs=(vmem, vmem),
+        scratch_shapes=[
+            pltpu.VMEM((H, Q), f32), pltpu.VMEM((H, Q), f32),
+            pltpu.VMEM((H, P_SIZE, Q), b16), pltpu.VMEM((H, Q, Q), b16), pltpu.VMEM((H, P_SIZE, Q), f32),
+            pltpu.VMEM((H, P_SIZE, Q), b16), pltpu.VMEM((H, P_SIZE, Q), b16), pltpu.VMEM((H, P_SIZE, Q), f32),
+            pltpu.VMEM((hp, Q), f32), pltpu.VMEM((n_tm, 8, N), f32),
+        ] + [states] * 8 + [dma((n_tm,))] * 10,
+        compiler_params=pltpu.CompilerParams(collective_id=1, has_side_effects=True, vmem_limit_bytes=60 * 1024 * 1024),
+    )(lg, weights, cum, valid, proj, proj_t, g_t, gain)
+
+
 def on_device(embeds, w_in, log_decay, clip_keep, clip_starts, valid_len, norm_gain, g_out):
     n_cam = lax.axis_size("cam")
     n_tm = lax.axis_size("tm")
     t_dev = embeds.shape[1]
-    groups = t_dev // Q
     x_rows = lax.all_to_all(embeds, "cam", split_axis=0, concat_axis=2, tiled=True)[0]
     projected = jnp.dot(x_rows, w_in, preferred_element_type=jnp.float32).astype(jnp.bfloat16)
     positions = lax.axis_index("tm") * t_dev + jnp.arange(t_dev, dtype=jnp.int32)
     is_start = jnp.any(positions[:, None] == clip_starts[0][None, :], axis=1)
     log_rates = log_decay[0] + jnp.where(is_start[None, :], jnp.log(clip_keep)[:, None], 0.0)
     valid_rows = (positions < valid_len[0]).astype(jnp.float32)
-    proj_float = projected.astype(jnp.float32)
-    x_blocks = (proj_float[:, :HP].reshape(t_dev, H, P_SIZE) * valid_rows[:, None, None]).reshape(
-        groups, Q, H, P_SIZE
-    )
-    b_blocks = proj_float[:, HP : HP + N].reshape(groups, Q, N)
-    c_blocks = proj_float[:, HP + N :].reshape(groups, Q, N)
-    cum_rate = jnp.cumsum(log_rates.reshape(H, groups, Q), axis=2).transpose(1, 0, 2)
-    group_log = cum_rate[:, :, -1]
-    causal = jnp.arange(Q)[:, None] >= jnp.arange(Q)[None, :]
-    gaps = cum_rate[:, :, :, None] - cum_rate[:, :, None, :]
+    cum_rate = jnp.cumsum(log_rates, axis=1)
+    lg = jnp.broadcast_to(cum_rate[:, -1][:, None, None], (H, 8, N))
+    causal = jnp.arange(Q)[:, None] <= jnp.arange(Q)[None, :]
+    gaps = cum_rate[:, None, :] - cum_rate[:, :, None]
     weights = jnp.where(causal, jnp.exp(jnp.where(causal, gaps, 0.0)), 0.0)
-    scores = jnp.einsum("ktn,ksn->kts", c_blocks, b_blocks, precision=precise)
-    mixing = weights * scores[:, None]
-    y_in = jnp.einsum("khts,kshp->kthp", mixing, x_blocks, precision=precise)
-    tail_decay = jnp.exp(group_log[:, :, None] - cum_rate).transpose(0, 2, 1)
-    lift_decay = jnp.exp(cum_rate).transpose(0, 2, 1)
-    local_state = jnp.einsum(
-        "kshp,ksn->khpn", x_blocks * tail_decay[:, :, :, None], b_blocks, precision=precise
-    )
-    zero_before = [jnp.zeros((H, P_SIZE, N), jnp.float32)]
-    zero_end = jnp.exp(group_log[-1])[:, None, None] * zero_before[-1] + local_state[-1]
-    block_log = jnp.sum(group_log, axis=0)
-    s_in = prefix_states(block_log, zero_end, False)
-    lead_log = jnp.cumsum(group_log, axis=0) - group_log
-    state_before = jnp.exp(lead_log)[:, :, None, None] * s_in[None] + jnp.stack(zero_before)
-    y_out = lift_decay[:, :, :, None] * jnp.einsum(
-        "khpn,ktn->kthp", state_before, c_blocks, precision=precise
-    )
-    raw_out = (y_in + y_out).reshape(t_dev, H, P_SIZE)
-    inv_rms = lax.rsqrt(jnp.mean(raw_out * raw_out, axis=-1, keepdims=True) + epsilon)
-    normed = raw_out * inv_rms
-    layer_out = (normed.reshape(t_dev, HP) * norm_gain[None, :] * valid_rows[:, None]).astype(
-        jnp.bfloat16
-    )
-    d_normed = (g_out[0].astype(jnp.float32) * norm_gain[None, :] * valid_rows[:, None]).reshape(
-        t_dev, H, P_SIZE
-    )
-    d_output = inv_rms * (d_normed - normed * jnp.mean(d_normed * normed, axis=-1, keepdims=True))
-    d_blocks = d_output.reshape(groups, Q, H, P_SIZE)
-    back_state = jnp.einsum(
-        "kthp,ktn->khpn", d_blocks * lift_decay[:, :, :, None], c_blocks, precision=precise
-    )
-    zero_after = [jnp.zeros((H, P_SIZE, N), jnp.float32)]
-    zero_start = jnp.exp(group_log[0])[:, None, None] * zero_after[0] + back_state[0]
-    r_out = prefix_states(block_log, zero_start, True)
-    trail_log = jnp.cumsum(group_log[::-1], axis=0)[::-1] - group_log
-    grad_after = jnp.exp(trail_log)[:, :, None, None] * r_out[None] + jnp.stack(zero_after)
-    d_inputs = jnp.einsum("khts,kthp->kshp", mixing, d_blocks, precision=precise)
-    d_inputs = d_inputs + tail_decay[:, :, :, None] * jnp.einsum(
-        "khpn,ksn->kshp", grad_after, b_blocks, precision=precise
-    )
-    pair_terms = weights * jnp.einsum("kthp,kshp->khts", d_blocks, x_blocks, precision=precise)
-    d_c = jnp.einsum("khts,ksn->ktn", pair_terms, b_blocks, precision=precise)
-    d_c = d_c + jnp.einsum(
-        "kthp,khpn->ktn", d_blocks * lift_decay[:, :, :, None], state_before, precision=precise
-    )
-    d_b = jnp.einsum("khts,ktn->ksn", pair_terms, c_blocks, precision=precise)
-    d_b = d_b + jnp.einsum(
-        "kshp,khpn->ksn", x_blocks * tail_decay[:, :, :, None], grad_after, precision=precise
-    )
-    du_rows = d_inputs.reshape(t_dev, HP) * valid_rows[:, None]
-    d_proj = jnp.concatenate(
-        [du_rows, d_b.reshape(t_dev, N), d_c.reshape(t_dev, N)], axis=1
-    ).astype(jnp.bfloat16)
+    keep = jnp.where(jnp.arange(HP + 2 * N)[None, :] < HP, valid_rows[:, None], 1.0)
+    proj = (projected.astype(jnp.float32) * keep).astype(jnp.bfloat16)
+    gain = jnp.broadcast_to(norm_gain[:, None], (HP, Q))
+    valid = jnp.broadcast_to(valid_rows[None, :], (8, Q))
+    layer_out, d_proj = scan_both(lg, weights, cum_rate, valid, proj, proj.T, g_out[0].T, gain)
     grad_scale = 1.0 / math.sqrt(n_cam * t_dev * n_tm)
     d_embeds, d_w_in = grads(d_proj, x_rows, w_in, grad_scale)
     return (layer_out[None], d_embeds, d_w_in)

time: 198 us -> 148 us (0.75)
  Pallas kernels: 45.3 us -> 102 us
  waiting for transfers between devices: 45 us -> 13.9 us
  matrix products: 36 us -> 6.74 us
  starting transfers between devices: 34 us -> 9 us
  local copies, waits for them, and re-layouts: 25.5 us -> 11.2 us
  other arithmetic: 9.44 us -> 4.12 us
    pallas_call x0 -> x1, Pallas kernels: none -> 54.6 us  [scan_both(): pl.pallas_call(scan_kernel, name='scan_both', out_shape=(jax.ShapeDtypeSt...]
    dot_general x14 -> x0, matrix products: 30.7 us -> none  [the longest x1 6.51 us: on_device(): y_in = jnp.einsum('khts,kshp->kthp', mixing, x_blocks, precision=precise)]
    all_to_all x4 -> x0, waiting for transfers between devices: 28.9 us -> none  [the longest x2 18.1 us: prefix_states(): mine = lax.all_to_all(packed, 'tm', split_axis=0, concat_axis=0, tiled=True)]
    all_to_all x4 -> x0, starting transfers between devices: 25 us -> none  [the longest x2 13.8 us: prefix_states(): mine = lax.all_to_all(packed, 'tm', split_axis=0, concat_axis=0, tiled=True)]
    slice x6 -> x1, local copies, waits for them, and re-layouts: 7.83 us -> 0.18 us  [on_device(): lg = jnp.broadcast_to(cum_rate[:, -1][:, None, None], (H, 8, N))]
    mul x6 -> x0, local copies, waits for them, and re-layouts: 5.75 us -> none  [the longest x2 3.72 us: on_device(): normed = raw_out * inv_rms]
    concatenate x3 -> x0, other arithmetic: 3.14 us -> none  [the longest x2 2.28 us: prefix_states(): packed = jnp.concatenate([state, extra], axis=1)]
    unnamed x31 -> x21, local copies, waits for them, and re-layouts: 9.08 us -> 6.43 us
  transfers between devices with their start and end apart: 5 -> 1, of which waited for: 4 -> 1; matrix products, arithmetic and copies ran while one was open for 16% -> 2% of each run, Pallas kernels for 0% -> 0%
where the time goes in v3:
time: 148 us
  Pallas kernels  102 us (69%)
  waiting for transfers between devices  13.9 us (9%)
  local copies, waits for them, and re-layouts  11.2 us (8%)
  starting transfers between devices  9 us (6%)
  matrix products  6.74 us (5%)
  other arithmetic  4.12 us (3%)
    pallas_call x1, Pallas kernels, scan_both(): pl.pallas_call(scan_kernel, name='scan_both', out_shape=(jax.ShapeDtypeSt...  54.6 us
    pallas_call x1, Pallas kernels, grads(): pl.pallas_call(functools.partial(grad_kernel, scale), name='grads', out_s...  47.1 us
    all_to_all x1, waiting for transfers between devices, on_device(): lax.all_to_all(embeds, 'cam', split_axis=0, concat_axis=2, tiled=True)[0]  13.9 us
    all_to_all x1, starting transfers between devices, on_device(): lax.all_to_all(embeds, 'cam', split_axis=0, concat_axis=2, tiled=True)[0]  9 us
    dot_general x1, matrix products, on_device(): jnp.dot(x_rows, w_in, preferred_element_type=jnp.float32)  6.74 us
    unnamed x21, local copies, waits for them, and re-layouts  6.43 us
  transfers between devices with their start and end apart: 1, of which 1 were waited for; matrix products, arithmetic and copies ran while one was open for 2% of the time, Pallas kernels for 0%

profile of v3, /device:TPU:1, one launch (start us, length us, event | category | flops | bytes accessed | tf_op | source)
XLA Modules:
  0.0 148.0 jit_solution(4924469742507075722)
XLA Ops:
  0.6 0.0 copy-start.6
  0.6 0.0 copy-start
  0.7 0.0 copy-start.7
  0.7 0.0 copy-start.4
  0.7 2.1 %copy.19 = bf16[8,128,256]{1,2,0:T(8,128)(2,1)} copy(bf16[8,128,256]{2,1,0:T(8,128)(2,1)} %param.8) | data formatting | bytes 1048576 | tf_op args[0]
  2.8 9.0 %all-to-all-start = ((bf16[8,128,256]{1,2,0:T(8,128)(2,1)}), bf16[8,128,256]{1,2,0:T(8,128)(2,1)S(1)}, u32[]{:S(2)}, u32[]{:S(2)}) async-start(bf16[8,128,256]{1,2,0:T(8,128)(2,1)} %copy.19), calls=%async_computation | async-start | bytes 1048576 | tf_op jit(solution)/shard_map/all_to_all | solution.py:409
  12.4 0.0 copy-done.6
  12.5 0.0 copy-done
  12.5 1.0 copy.21
  13.5 0.0 copy-done.7
  13.5 0.1 compare_reduce_fusion
  13.6 0.0 copy-done.4
  13.6 0.1 bitcast_add_fusion
  13.6 0.3 reduce_window_sum.11.cum_ref
  14.0 0.2 slice_reduce_fusion
  14.1 1.7 %exponential_select_fusion.w_ref = f32[32,128,128]{2,1,0:T(8,128)} fusion(f32[32,128]{1,0:T(8,128)S(1)} %reduce_window_sum.11.cum_ref, pred[128,128]{1,0:T(8,128)(4,1)S(1)} %iota_compare_fusion), kind=kLoop, calls=%fused_computation.2 | loop fusion | flops 1572864 | bytes 2129920 | tf_op jit(solution)/shard_map/jit(_where)/select_n | solution.py:419
  15.9 13.9 %all-to-all-done = bf16[8,128,256]{1,2,0:T(8,128)(2,1)S(1)} async-done(((bf16[8,128,256]{1,2,0:T(8,128)(2,1)}), bf16[8,128,256]{1,2,0:T(8,128)(2,1)S(1)}, u32[]{:S(2)}, u32[]{:S(2)}) %all-to-all-start) | async-done | bytes 524320 | tf_op jit(solution)/shard_map/all_to_all | solution.py:409
  29.7 0.8 copy.23
  30.6 6.7 %multiply_convert_fusion = (bf16[128,2304]{0,1:T(8,128)(2,1)S(1)}, f32[128,2304]{0,1:T(8,128)S(1)}) fusion(f32[128]{0:T(128)S(1)} %compare_convert_fusion, pred[2304]{0:T(1024)(128)(4,1)S(1)} %iota_compare_fusion.1, bf16[128,2048]{0,1:T(8,128)(2,1)S(1)} %bitcast.28, bf16[2048,2304]{1,0:T(8,128)(2,1)} %w_ref.1), kind=kOutput, calls=%fused_computation.5 | convolution fusion | flops 1209434112 | bytes 11733760 | tf_op jit(solution)/shard_map/dot_general | solution.py:410
  37.3 0.0 copy-done.2
  37.3 0.0 copy-start.5
  37.3 1.1 copy.22.proj_ref
  38.4 1.9 %fusion.1.xt_ref = bf16[2304,128]{1,0:T(8,128)(2,1)} fusion(f32[128,2304]{0,1:T(8,128)S(1)} %get-tuple-element.12, f32[128]{0:T(128)S(1)} %compare_convert_fusion, pred[2304]{0:T(1024)(128)(4,1)S(1)} %iota_compare_fusion.1), kind=kLoop, calls=%fused_computation.4 | loop fusion | flops 884736 | bytes 1772288 | tf_op jit(solution)/shard_map/convert_element_type | solution.py:421
  40.3 0.6 broadcast_in_dim.96.valid_ref
  40.9 0.8 broadcast_in_dim.93.lg_ref
  41.7 1.3 broadcast_in_dim.103.gain_ref
  43.0 54.6 %scan_both.1 = (bf16[128,2048]{1,0:T(8,128)(2,1)}, bf16[128,2304]{1,0:T(8,128)(2,1)}) custom-call(f32[32,8,128]{2,1,0:T(8,128)} %broadcast_in_dim.93.lg_ref, f32[32,128,128]{2,1,0:T(8,128)} %exponential_select_fusion.w_ref, f32[32,128]{1,0:T(8,128)} %copy-done.2, f32[8,128]{1,0:T(8,128)} %broadcast_in_dim.96.valid_ref, bf16[128,2304]{1,0:T(8,128)(2,1)} %copy.22.proj_ref, ...), custom_call_target="tpu_custom_call" | custom-call | tf_op jit(solution)/shard_map/scan_both/pallas_call | solution.py:389
  97.7 0.0 copy-start.1
  97.7 47.1 %grads.1 = (bf16[8,128,256]{2,1,0:T(8,128)(2,1)}, f32[8,2304]{1,0:T(8,128)}) custom-call(bf16[128,2304]{1,0:T(8,128)(2,1)} %get-tuple-element.8.dp_ref, bf16[4,4,128,128]{3,2,1,0:T(8,128)(2,1)} %bitcast.29, bf16[2048,2304]{1,0:T(8,128)(2,1)} %w_ref.1), custom_call_target="tpu_custom_call" | custom-call | tf_op jit(solution)/shard_map/grads/pallas_call | solution.py:193
  144.7 0.8 copy.29
  145.5 1.9 %copy.30 = bf16[8,128,256]{2,1,0:T(8,128)(2,1)} copy(bf16[8,128,256]{2,1,0:T(8,128)(2,1)} %get-tuple-element.17) | data formatting | bytes 1048576
  147.4 0.6 copy.31
  (10 shorter events, 0.0 us)
Async XLA Ops:
  0.6 11.8 %copy-start.6 = (f32[32]{0:T(128)S(1)}, f32[32]{0:T(128)}, u32[]{:S(2)}) copy-start(f32[32]{0:T(128)} %param.11) | copy-start | bytes 388
  0.6 11.8 %copy-start = (bf16[1,128,2048]{2,1,0:T(8,128)(2,1)S(1)}, bf16[1,128,2048]{2,1,0:T(8,128)(2,1)}, u32[]{:S(2)}) copy-start(bf16[1,128,2048]{2,1,0:T(8,128)(2,1)} %param.15) | copy-start | bytes 1572868
  0.7 12.8 %copy-start.7 = (s32[1,3]{1,0:T(1,128)S(1)}, s32[1,3]{1,0:T(1,128)}, u32[]{:S(2)}) copy-start(s32[1,3]{1,0:T(1,128)} %param.12) | copy-start | bytes 40
  0.7 12.9 %copy-start.4 = (f32[1,32,128]{2,1,0:T(8,128)S(1)}, f32[1,32,128]{2,1,0:T(8,128)}, u32[]{:S(2)}) copy-start(f32[1,32,128]{2,1,0:T(8,128)} %param.10) | copy-start | bytes 49156
  2.8 27.0 %all-to-all-start = ((bf16[8,128,256]{1,2,0:T(8,128)(2,1)}), bf16[8,128,256]{1,2,0:T(8,128)(2,1)S(1)}, u32[]{:S(2)}, u32[]{:S(2)}) async-start(bf16[8,128,256]{1,2,0:T(8,128)(2,1)} %copy.19), calls=%async_computation | async-start | bytes 1048576 | tf_op jit(solution)/shard_map/all_to_all | solution.py:409
  13.9 23.4 %copy-start.2 = (f32[32,128]{1,0:T(8,128)}, f32[32,128]{1,0:T(8,128)S(1)}, u32[]{:S(2)}) copy-start(f32[32,128]{1,0:T(8,128)S(1)} %reduce_window_sum.11.cum_ref) | copy-start | bytes 49156
  37.3 4.4 %copy-start.5 = (f32[2048]{0:T(1024)S(1)}, f32[2048]{0:T(1024)}, u32[]{:S(2)}) copy-start(f32[2048]{0:T(1024)} %param.14) | copy-start | bytes 24580
  97.7 47.1 %copy-start.1 = (bf16[128,2048]{1,0:T(8,128)(2,1)S(1)}, bf16[128,2048]{1,0:T(8,128)(2,1)}, u32[]{:S(2)}) copy-start(bf16[128,2048]{1,0:T(8,128)(2,1)} %get-tuple-element.7) | copy-start | bytes 1572868
  144.7 2.7 %copy-start.3 = (f32[8,2304]{1,0:T(8,128)S(1)}, f32[8,2304]{1,0:T(8,128)}, u32[]{:S(2)}) copy-start(f32[8,2304]{1,0:T(8,128)} %get-tuple-element.18) | copy-start | bytes 221188

commit v4 on v1

v4 whole, which is shorter than its diff:
```python
import functools
import math

import jax
import jax.numpy as jnp
from jax import lax
from jax.experimental import pallas as pl
from jax.experimental.pallas import tpu as pltpu
from jax.sharding import PartitionSpec as P

D = 2048
H = 32
P_SIZE = 64
N = 128
Q = 128
HP = 2048
NCLIP = 3


epsilon = 1e-05
MESH = pl.DeviceIdType.MESH
NX, NY, NZ = 4, 4, 8


def at(x, y, z, core):
    return (z, (x * NY + y) * 2 + core)


def send(src, dst, sem_a, sem_b, peer):
    return pltpu.make_async_remote_copy(
        src_ref=src, dst_ref=dst, send_sem=sem_a, recv_sem=sem_b, device_id=peer, device_id_type=MESH
    )


def loop(start, end, body):
    def step(k, _):
        body(k)
        return 0
    lax.fori_loop(start, end, step, 0)


def layer_kernel(scale, starts_ref, len_ref, emb_ref, w_ref, rate_ref, keep_ref, gain_ref, g_ref,
                 out_ref, demb_ref, dw_ref,
                 wv, xin, acc, proj, xt, xtp, gt, gain, wts, cum, tail, lift, tot,
                 xw, mix, yin, dt, dl, din, lot, lg, lgot, snd1, got1, snd2, sin, snd3, got3, snd4, rin,
                 dp, xg, pg, rows_out, s2, r2, s3, r3, own,
                 w_sem, a_send, a_recv,
                 l_send, l_recv, send1, recv1, send2, recv2, send3, recv3, send4, recv4,
                 x_send, x_recv, p_send, p_recv, e_send, e_recv, send5, recv5, send6, recv6):
    f32, b16 = jnp.float32, jnp.bfloat16
    me, z = lax.axis_index("tm"), lax.axis_index("cam")
    n_tm = 2 * NX * NY
    x, y, core = me // (2 * NY), (me // 2) % NY, me % 2
    hp = H * P_SIZE
    width = emb_ref.shape[2]
    half = dp.shape[1] // 2
    group = 4

    def w_copy(j):
        c = (z + NZ - 1 - j) % NZ
        return pltpu.make_async_copy(w_ref.at[pl.ds(pl.multiple_of(c * width, width), width)], wv.at[c], w_sem.at[j])

    barrier = pltpu.get_barrier_semaphore()

    def greet(peer):
        pl.semaphore_signal(barrier, inc=1, device_id=peer, device_id_type=MESH)

    loop(1, NZ, lambda j: greet(((z + j) % NZ, me)))
    loop(1, NZ, lambda j: greet(((z + j) % NZ, me + 1 - 2 * core)))
    loop(1, n_tm, lambda j: greet((z, (me + j) % n_tm)))
    for j in (7, 0, 6, 1, 5, 2, 4, 3):
        w_copy(j).start()

    def dot(a, b):
        return jnp.dot(a, b, preferred_element_type=f32)

    def dot_t(a, b):
        return lax.dot_general(a, b, (((1,), (1,)), ((), ())), preferred_element_type=f32)

    def t_dot(a, b):
        return lax.dot_general(a, b, (((0,), (0,)), ((), ())), preferred_element_type=f32)

    def lanes_of(shape):
        return lax.broadcasted_iota(jnp.int32, shape, len(shape) - 1)

    def subs_of(shape):
        return lax.broadcasted_iota(jnp.int32, shape, 0)

    base = me * Q
    here = lanes_of((1, Q)) + base
    is_start = here == starts_ref[0, 0]
    for k in range(1, NCLIP):
        is_start = is_start | (here == starts_ref[0, k])
    keep_log = jnp.log(keep_ref[...])
    keep_col = jnp.sum(jnp.where(lanes_of((H, H)) == subs_of((H, H)), keep_log, 0.0), axis=1, keepdims=True)
    rates = rate_ref[0] + jnp.where(is_start, keep_col, 0.0)
    upper = (subs_of((Q, Q)) <= lanes_of((Q, Q)))
    running = jnp.dot(rates, upper.astype(f32), precision=lax.Precision.HIGHEST, preferred_element_type=f32)
    cum[...] = running
    tail[...] = jnp.exp(running[:, Q - 1:Q] - running)
    lift[...] = jnp.exp(running)
    tot[...] = jnp.broadcast_to(running[:, Q - 1:Q], (H, Q))
    valid = (here < len_ref[0]).astype(f32)
    valid_col = (subs_of((Q, Q)) + base < len_ref[0])

    def logs_of(h):
        lg[h] = jnp.broadcast_to(tot[pl.ds(h, 1)], (8, Q))

    loop(0, H, logs_of)

    pl.semaphore_wait(barrier, 2 * (NZ - 1) + n_tm - 1)

    def a_copy(j):
        lanes = pl.ds(pl.multiple_of(z * width, width), width)
        return send(emb_ref.at[(z + 1 + j) % NZ], xin.at[:, lanes], a_send.at[j], a_recv.at[j], ((z + 1 + j) % NZ, me))

    def block(c):
        return xin.at[:, pl.ds(pl.multiple_of(c * width, width), width)]

    a_home = pltpu.make_async_copy(emb_ref.at[z], block(z), a_recv.at[NZ - 1])
    for j in (3, 2, 4, 1, 5, 0, 6):
        a_copy(j).start()
    a_home.start()

    def exchange(src, dst, sem_a, sem_b):
        def copy(j):
            peer = (me + j) % n_tm
            return send(src.at[peer], dst.at[me], sem_a.at[j], sem_b.at[j], (z, peer))

        def start():
            loop(1, n_tm, lambda j: copy(j).start())
            dst[me] = src[me]

        return (start, lambda: loop(1, n_tm, lambda j: copy(j).wait_recv()),
                lambda: loop(1, n_tm, lambda j: copy(j).wait_send()))

    logs = exchange(lg, lgot, l_send, l_recv)
    fwd_out = exchange(snd1, got1, send1, recv1)
    fwd_back = exchange(snd2, sin, send2, recv2)
    bwd_out = exchange(snd3, got3, send3, recv3)
    bwd_back = exchange(snd4, rin, send4, recv4)
    logs[0]()

    def weights_of(h):
        row = jnp.broadcast_to(cum[pl.ds(h, 1)], (Q, Q))
        wts[h] = jnp.where(upper, jnp.exp(jnp.where(upper, row - row.T, 0.0)), 0.0)

    loop(0, H, weights_of)

    def columns_of(k):
        part = pl.ds(pl.multiple_of(k * Q, Q), Q)
        gt[part] = g_ref[0, :, part].astype(f32).T.astype(b16)
        gain[part] = jnp.broadcast_to(gain_ref[pl.ds(k, 1)], (Q, Q)).T * valid

    loop(0, hp // Q, columns_of)

    piece = Q // (2 * NY)
    for n, j in enumerate((7, 0, 6, 1, 5, 2, 4, 3)):
        c = (z + NZ - 1 - j) % NZ
        w_copy(j).wait()
        if j == NZ - 1:
            a_home.wait()
            c = z
        else:
            a_copy(j).wait_recv()
        got = block(c)[...]
        term = dot(got, wv[c])
        if n == 0:
            acc[...] = term
        else:
            acc[...] += term
        for k in range(width // Q):
            turned = got[:, k * Q:(k + 1) * Q].astype(f32).T.astype(b16)
            for m in range(Q // piece):
                feature = k * Q + m * piece
                xtp[feature // (NY * piece), (feature // piece) % NY, pl.ds(pl.multiple_of(c * piece, piece), piece)] = (
                    turned[m * piece:(m + 1) * piece])

    def part_of(color):
        return dp.at[:, pl.ds(color * half, half)]

    def lanes(slot):
        return xg.at[:, :, pl.ds(pl.multiple_of(slot * Q, Q), Q)]

    def x_line(j):
        k, slot = (x + j) % NX, x * 2 + core
        peer = at(k, y, z, 0)
        return (send(xtp.at[k], lanes(slot), x_send.at[0, j], x_recv.at[slot], peer),
                send(part_of(0), pg.at[slot], p_send.at[0, j], p_recv.at[slot], peer))

    def y_line(j):
        k, slot = (y + j) % NY, y * 2 + core
        peer = at(x, k, z, 1)
        return (send(xtp.at[:, k], lanes(slot), x_send.at[1, j], x_recv.at[slot], peer),
                send(part_of(1), pg.at[slot], p_send.at[1, j], p_recv.at[slot], peer))

    def lines(what, act):
        for j in (2, 1, 3):
            act(x_line(j)[what])
            act(y_line(j)[what])

        @pl.when(core == 0)
        def _():
            act(y_line(0)[what])

        @pl.when(core == 1)
        def _():
            act(x_line(0)[what])

    lines(0, lambda copy: copy.start())

    @pl.when(core == 0)
    def _():
        pltpu.make_async_copy(xtp.at[x], lanes(x * 2), x_recv.at[x * 2]).start()

    @pl.when(core == 1)
    def _():
        pltpu.make_async_copy(xtp.at[:, y], lanes(y * 2 + 1), x_recv.at[y * 2 + 1]).start()

    for k in range((hp + 2 * N) // Q):
        part = acc[:, k * Q:(k + 1) * Q]
        if k < hp // Q:
            part = jnp.where(valid_col, part, 0.0)
        proj[:, k * Q:(k + 1) * Q] = part.astype(b16)
        xt[k * Q:(k + 1) * Q] = part.T.astype(b16)

    b_nat, c_nat = proj[:, hp:hp + N], proj[:, hp + N:hp + 2 * N]
    b_t, c_t = xt[hp:hp + N], xt[hp + N:hp + 2 * N]

    def rows(g, i):
        return pl.ds(pl.multiple_of((g * group + i) * P_SIZE, P_SIZE), P_SIZE)

    def local_states(g):
        for i in range(group):
            h = g * group + i
            xw[h] = (xt[rows(g, i)].astype(f32) * tail[pl.ds(h, 1)]).astype(b16)
        states = dot(xw[pl.ds(g * group, group)].reshape(group * P_SIZE, Q), b_nat)
        snd1[pl.ds(g * group, group)] = states.astype(b16).reshape(group, P_SIZE, N)

    loop(0, H // group, local_states)
    fwd_out[0]()

    scores = dot(b_nat, c_t)

    def inside(g):
        for i in range(group):
            h = g * group + i
            mix[h] = (wts[h] * scores).astype(b16)
            yin[h] = dot(xt[rows(g, i)], mix[h])

    loop(0, H // group, inside)
    logs[1]()
    fwd_out[1]()

    def scan(parts, out, reverse):
        def body(k, state):
            i = n_tm - 1 - k if reverse else k
            out[i] = state.astype(b16).reshape(P_SIZE, N)
            decay = jnp.exp(lgot[i])
            return decay[None] * state + parts[i].astype(f32).reshape(P_SIZE // 8, 8, N)
        lax.fori_loop(0, n_tm, body, jnp.zeros((P_SIZE // 8, 8, N), f32))

    scan(got1, snd2, False)
    fwd_back[0]()
    fwd_back[1]()

    def norm_step(g):
        carried = dot(sin[pl.ds(g * group, group)].reshape(group * P_SIZE, N), c_t)
        for i in range(group):
            h = g * group + i
            up = lift[pl.ds(h, 1)]
            raw = yin[h] + up * carried[i * P_SIZE:(i + 1) * P_SIZE]
            inv = lax.rsqrt(jnp.mean(raw * raw, axis=0, keepdims=True) + epsilon)
            normed = raw * inv
            scaled = gain[rows(g, i)]
            lot[rows(g, i)] = normed * scaled
            d_normed = gt[rows(g, i)].astype(f32) * scaled
            d_out = inv * (d_normed - normed * jnp.mean(d_normed * normed, axis=0, keepdims=True))
            dt[h] = d_out.astype(b16)
            dl[h] = (d_out * up).astype(b16)
        states = dot(dl[pl.ds(g * group, group)].reshape(group * P_SIZE, Q), c_nat)
        snd3[pl.ds(g * group, group)] = states.astype(b16).reshape(group, P_SIZE, N)

    loop(0, H // group, norm_step)
    bwd_out[0]()

    first = subs_of((2 * P_SIZE, Q)) < P_SIZE

    def pairs(g, total):
        for i in range(0, group, 2):
            h = g * group + i
            d_two = dt[pl.ds(h, 2)].reshape(2 * P_SIZE, Q)
            zero = jnp.zeros_like(d_two)
            spread = jnp.concatenate([jnp.where(first, d_two, zero), jnp.where(first, zero, d_two)], axis=1)
            x_two = proj[:, pl.ds(pl.multiple_of(h * P_SIZE, 2 * P_SIZE), 2 * P_SIZE)]
            both = dot(x_two, spread)
            total = total + wts[h] * both[:, :Q] + wts[h + 1] * both[:, Q:]
            din[h] = dot_t(dt[h], mix[h])
            din[h + 1] = dot_t(dt[h + 1], mix[h + 1])
        return total

    pair_sum = lax.fori_loop(0, H // group, pairs, jnp.zeros((Q, Q), f32)).astype(b16)
    bwd_out[1]()
    scan(got3, snd4, True)
    bwd_back[0]()
    d_c = t_dot(pair_sum, b_nat) + t_dot(dl[...].reshape(hp, Q), sin[...].reshape(hp, N))
    d_b = dot(pair_sum, c_nat)
    dp[:, hp + N:hp + 2 * N] = d_c.astype(b16)
    for k in range(hp // Q):
        out_ref[:, k * Q:(k + 1) * Q] = lot[k * Q:(k + 1) * Q].T.astype(b16)
    bwd_back[1]()
    d_b = d_b + t_dot(xw[...].reshape(hp, Q), rin[...].reshape(hp, N))
    dp[:, hp:hp + N] = d_b.astype(b16)
    for k in range(H // 2):
        after = dot(rin[2 * k:2 * k + 2].reshape(2 * P_SIZE, N), b_t)
        two = [din[2 * k + i] + tail[2 * k + i:2 * k + i + 1] * after[i * P_SIZE:(i + 1) * P_SIZE] for i in range(2)]
        dp[:, k * Q:(k + 1) * Q] = (jnp.concatenate(two, axis=0) * valid).T.astype(b16)

    lines(1, lambda copy: copy.start())

    @pl.when(core == 0)
    def _():
        pltpu.make_async_copy(part_of(0), pg.at[x * 2], p_recv.at[x * 2]).start()

    @pl.when(core == 1)
    def _():
        pltpu.make_async_copy(part_of(1), pg.at[y * 2 + 1], p_recv.at[y * 2 + 1]).start()

    def e_copy(j):
        return send(rows_out.at[j], demb_ref.at[z], e_send.at[j], e_recv.at[j], ((z + 1 + j) % NZ, me))

    e_home = pltpu.make_async_copy(rows_out.at[NZ - 1], demb_ref.at[z], e_recv.at[NZ - 1])
    for j in (3, 2, 4, 1, 5, 0, 6, 7):
        rows_out[j] = dot_t(dp[...], wv[(z + 1 + j) % NZ]).astype(b16)
        if j < NZ - 1:
            e_copy(j).start()
        else:
            e_home.start()

    for slot in range(8):
        pltpu.make_async_copy(xtp.at[0], lanes(slot), x_recv.at[slot]).wait()
        pltpu.make_async_copy(part_of(0), pg.at[slot], p_recv.at[slot]).wait()

    p = (1 - core) * y + core * x

    def second(j):
        k = (p + 1 + j) % NX
        peer = at((1 - core) * x + core * k, (1 - core) * k + core * y, z, core)
        return send(s2.at[j], r2.at[j], send5.at[j], recv5.at[j], peer)

    right = pg[...].reshape(8 * Q, half)
    for j in (1, 0, 2, 3):
        part = dot(xg[(p + 1 + j) % NX], right)
        if j < NX - 1:
            s2[j] = part.astype(b16)
            second(j).start()
        else:
            own[...] = part
    for j in range(NX - 1):
        second(j).wait_recv()
    own[...] = (own[...] + r2[0].astype(f32) + r2[1].astype(f32) + r2[2].astype(f32)) * scale
    line = z * 2 + core
    for slot in range(2 * NZ):
        s3[slot] = own[8 * slot:8 * slot + 8].astype(b16)

    def third(j):
        slot = (line + j) % (2 * NZ)
        return send(s3.at[slot], r3.at[line], send6.at[j], recv6.at[line], at(x, y, slot // 2, slot % 2))

    def third_arrival(j):
        slot = (line + j) % (2 * NZ)
        return send(s3.at[0], r3.at[slot], send6.at[j], recv6.at[slot], at(x, y, slot // 2, slot % 2))

    for j in (8, 7, 9, 6, 10, 5, 11, 4, 12, 3, 13, 2, 14, 1, 15):
        third(j).start()
    r3[line] = s3[line]
    for j in range(1, 2 * NZ):
        third_arrival(j).wait_recv()
    for color in range(2):
        sums = r3[color].astype(f32)
        for c in range(1, NZ):
            sums = sums + r3[2 * c + color].astype(f32)
        dw_ref[:, color * half:(color + 1) * half] = sums

    for j in range(NZ - 1):
        a_copy(j).wait_send()
        e_copy(j).wait_send()
        e_copy(j).wait_recv()
    e_home.wait()
    for _, _, sent in (logs, fwd_out, fwd_back, bwd_out, bwd_back):
        sent()
    lines(0, lambda copy: copy.wait_send())
    lines(1, lambda copy: copy.wait_send())
    for j in range(NX - 1):
        second(j).wait_send()
    for j in range(1, 2 * NZ):
        third(j).wait_send()


def on_device(embeds, w_in, log_decay, clip_keep, clip_starts, valid_len, norm_gain, g_out):
    n_cam, t, width = embeds.shape
    d, e = w_in.shape
    n_tm = lax.axis_size("tm")
    half, part = e // 2, d // NX // NY
    scale = 1.0 / math.sqrt(n_cam * t * n_tm)
    dma = pltpu.SemaphoreType.DMA
    vmem = pl.BlockSpec(memory_space=pltpu.VMEM)
    smem = pl.BlockSpec(memory_space=pltpu.SMEM)
    hbm = pl.BlockSpec(memory_space=pl.ANY)
    f32, b16 = jnp.float32, jnp.bfloat16
    scratch = lambda dtype, *shape: pltpu.VMEM(shape, dtype)
    layer_out, d_embeds, d_w_in = pl.pallas_call(
        functools.partial(layer_kernel, scale),
        name="layer",
        out_shape=(jax.ShapeDtypeStruct((t, HP), b16), jax.ShapeDtypeStruct((n_cam, t, width), b16),
                   jax.ShapeDtypeStruct((part // n_cam // 2, e), f32)),
        in_specs=[smem, smem, hbm, hbm, vmem, vmem, vmem, vmem],
        out_specs=(vmem, hbm, vmem),
        scratch_shapes=[
            scratch(b16, n_cam, width, e), scratch(b16, t, d), scratch(f32, t, e), scratch(b16, t, e), scratch(b16, e, t),
            scratch(b16, NX, NY, part, t), scratch(b16, HP, t), scratch(f32, HP, t), scratch(f32, H, t, t),
            scratch(f32, H, t), scratch(f32, H, t), scratch(f32, H, t), scratch(f32, H, t),
            scratch(b16, H, P_SIZE, t), scratch(b16, H, t, t), scratch(f32, H, P_SIZE, t),
            scratch(b16, H, P_SIZE, t), scratch(b16, H, P_SIZE, t), scratch(f32, H, P_SIZE, t),
            scratch(f32, HP, t), scratch(f32, H, 8, N), scratch(f32, n_tm, 8, N),
        ] + [scratch(b16, n_tm, P_SIZE, N)] * 8 + [
            scratch(b16, t, e), scratch(b16, NX, part, 8 * t), scratch(b16, 8, t, half), scratch(b16, n_cam, t, width),
            scratch(b16, NX - 1, part, half), scratch(b16, NX - 1, part, half),
            scratch(b16, 2 * n_cam, part // n_cam // 2, half), scratch(b16, 2 * n_cam, part // n_cam // 2, half),
            scratch(f32, part, half),
            dma((n_cam,)), dma((n_cam,)), dma((n_cam,)),
        ] + [dma((n_tm,))] * 10 + [
            dma((2, NX)), dma((8,)), dma((2, NX)), dma((8,)), dma((n_cam,)), dma((n_cam,)),
            dma((NX,)), dma((NX,)), dma((2 * n_cam,)), dma((2 * n_cam,)),
        ],
        compiler_params=pltpu.CompilerParams(collective_id=0, has_side_effects=True, vmem_limit_bytes=60 * 1024 * 1024),
    )(clip_starts, valid_len, embeds, w_in, log_decay, clip_keep.reshape(1, H), norm_gain.reshape(HP // Q, Q), g_out)
    return (layer_out[None], d_embeds, d_w_in)


def solution(mesh):
    return jax.shard_map(
        on_device,
        mesh=mesh,
        in_specs=(
            P(None, "tm", "cam"),
            P(),
            P("cam", None, "tm"),
            P(),
            P("cam", None),
            P("cam"),
            P(),
            P("cam", "tm", None),
        ),
        out_specs=(P("cam", "tm", None), P(None, "tm", "cam"), P(("cam", "tm"), None)),
        check_vma=False,
    )
```

time: 302 us -> 119 us (0.39)
  waiting for transfers between devices: 181 us -> 0 us
  Pallas kernels: 0 us -> 112 us
  matrix products: 46 us -> 0 us
  starting transfers between devices: 32.1 us -> 0 us
  between operations: 15.1 us -> 1.29 us
  local copies, waits for them, and re-layouts: 17 us -> 5.27 us
  other arithmetic: 8.47 us -> 0 us
    pallas_call x0 -> x1, Pallas kernels: none -> 112 us  [on_device(): pl.pallas_call(functools.partial(layer_kernel, scale), name='layer', out_...]
    unnamed x3 -> x0, waiting for transfers between devices: 77.7 us -> none
    all_to_all x5 -> x0, waiting for transfers between devices: 51.9 us -> none  [the longest x2 30.3 us: prefix_states(): mine = lax.all_to_all(packed, 'tm', split_axis=0, concat_axis=0, tiled=True)]
    all_gather x1 -> x0, waiting for transfers between devices: 51.8 us -> none  [on_device(): all_proj = lax.all_gather(d_proj, 'cam').reshape(n_cam * t_dev, HP + 2 * N)]
    dot_general x17 -> x0, matrix products: 46 us -> none  [the longest x1 6.51 us: on_device(): y_in = jnp.einsum('khts,kshp->kthp', mixing, x_blocks, precision=precise)]
    all_to_all x5 -> x0, starting transfers between devices: 32.1 us -> none  [the longest x2 13.9 us: prefix_states(): mine = lax.all_to_all(packed, 'tm', split_axis=0, concat_axis=0, tiled=True)]
    slice x6 -> x0, local copies, waits for them, and re-layouts: 7.86 us -> none  [the longest x2 2.67 us: prefix_states(): parts = mine[:, :P_SIZE].reshape(size, P_SIZE * N)]
    concatenate x4 -> x0, other arithmetic: 3.29 us -> none  [the longest x2 2.29 us: prefix_states(): packed = jnp.concatenate([state, extra], axis=1)]
  transfers between devices with their start and end apart: 7 -> 0, of which waited for: 7 -> 0; matrix products, arithmetic and copies ran while one was open for 11% -> 0% of each run, Pallas kernels for 0% -> 0%
where the time goes in v4:
time: 119 us
  Pallas kernels  112 us (94%)
  local copies, waits for them, and re-layouts  5.27 us (4%)
  between operations  1.29 us (1%)
    pallas_call x1, Pallas kernels, on_device(): pl.pallas_call(functools.partial(layer_kernel, scale), name='layer', out_...  112 us
    unnamed x3, local copies, waits for them, and re-layouts  5.27 us

profile of v4, /device:TPU:1, one launch (start us, length us, event | category | flops | bytes accessed | tf_op | source)
XLA Modules:
  0.0 118.9 jit_solution(2496482557627204085)
XLA Ops:
  1.3 112.3 %layer.1 = (bf16[128,2048]{1,0:T(8,128)(2,1)}, bf16[8,128,256]{2,1,0:T(8,128)(2,1)}, f32[8,2304]{1,0:T(8,128)}) custom-call(s32[1,3]{1,0:T(1,128)} %starts_ref.1, s32[1]{0:T(128)S(6)} %copy.14.len_ref, bf16[8,128,256]{2,1,0:T(8,128)(2,1)} %emb_ref.1, bf16[2048,2304]{1,0:T(8,128)(2,1)} %w_ref.1, f32[1,32,128]{2,1,0:T(8,128)} %rate_ref.1, f32[1,32]{1,0:T(1,128)} %bitcast.5, ...), custom_call_target="tpu_custom_call" | custom-call | tf_op jit(solution)/shard_map/layer/pallas_call | solution.py:412
  113.6 1.9 %copy.15 = bf16[1,128,2048]{2,1,0:T(8,128)(2,1)} copy(bf16[1,128,2048]{2,1,0:T(8,128)(2,1)} %bitcast.3) | data formatting | bytes 1048576
  115.5 1.9 %copy.16 = bf16[8,128,256]{2,1,0:T(8,128)(2,1)} copy(bf16[8,128,256]{2,1,0:T(8,128)(2,1)} %get-tuple-element.13) | data formatting | bytes 1048576
  117.4 1.5 %copy.17 = f32[8,2304]{1,0:T(8,128)} copy(f32[8,2304]{1,0:T(8,128)} %get-tuple-element.14) | data formatting | bytes 147456

commit v5 on v4

--- a/solution.py
+++ b/solution.py
@@ -20,6 +20,8 @@
 epsilon = 1e-05
 MESH = pl.DeviceIdType.MESH
 NX, NY, NZ = 4, 4, 8
+PIECES = 2
+COLUMNS = ((0, 512), (512, 640))
 
 
 def at(x, y, z, core):
@@ -43,8 +45,8 @@
                  out_ref, demb_ref, dw_ref,
                  wv, xin, acc, proj, xt, xtp, gt, gain, wts, cum, tail, lift, tot,
                  xw, mix, yin, dt, dl, din, lot, lg, lgot, snd1, got1, snd2, sin, snd3, got3, snd4, rin,
-                 dp, xg, pg, rows_out, s2, r2, s3, r3, own,
-                 w_sem, a_send, a_recv,
+                 dp, xg, pg, rows_out, s2, r2, s3, r3, own, lay,
+                 w_sem, o_sem, a_send, a_recv,
                  l_send, l_recv, send1, recv1, send2, recv2, send3, recv3, send4, recv4,
                  x_send, x_recv, p_send, p_recv, e_send, e_recv, send5, recv5, send6, recv6):
     f32, b16 = jnp.float32, jnp.bfloat16
@@ -122,23 +124,37 @@
         a_copy(j).start()
     a_home.start()
 
-    def exchange(src, dst, sem_a, sem_b):
+    def apart(i):
+        return (2 + 3 * i + 3 * (i // 2) + 2 * (i // 3)) % 4
+
+    def exchange(src, dst, sem_a, sem_b, part=None):
         def copy(j):
-            peer = (me + j) % n_tm
-            return send(src.at[peer], dst.at[me], sem_a.at[j], sem_b.at[j], (z, peer))
+            dx, dy = apart(j // (2 * NY)), apart((j // 2) % NY)
+            peer = (((x + dx) % NX) * NY + (y + dy) % NY) * 2 + (core + 1 + j) % 2
+            if part is None:
+                return send(src.at[peer], dst.at[me], sem_a.at[j], sem_b.at[j], (z, peer))
+            return send(src.at[peer, part], dst.at[me, part], sem_a.at[j], sem_b.at[j], (z, peer))
 
         def start():
-            loop(1, n_tm, lambda j: copy(j).start())
-            dst[me] = src[me]
-
-        return (start, lambda: loop(1, n_tm, lambda j: copy(j).wait_recv()),
-                lambda: loop(1, n_tm, lambda j: copy(j).wait_send()))
+            loop(0, n_tm - 1, lambda j: copy(j).start())
+            if part is None:
+                dst[me] = src[me]
+            else:
+                dst[me, part] = src[me, part]
+
+        return (start, lambda: loop(0, n_tm - 1, lambda j: copy(j).wait_recv()),
+                lambda: loop(0, n_tm - 1, lambda j: copy(j).wait_send()))
+
+    pieces = [pl.ds(k * (P_SIZE // PIECES), P_SIZE // PIECES) for k in range(PIECES)]
+
+    def exchanges(src, dst, sem_a, sem_b):
+        return [exchange(src, dst, sem_a.at[k], sem_b.at[k], piece) for k, piece in enumerate(pieces)]
 
     logs = exchange(lg, lgot, l_send, l_recv)
-    fwd_out = exchange(snd1, got1, send1, recv1)
-    fwd_back = exchange(snd2, sin, send2, recv2)
-    bwd_out = exchange(snd3, got3, send3, recv3)
-    bwd_back = exchange(snd4, rin, send4, recv4)
+    fwd_out = exchanges(snd1, got1, send1, recv1)
+    fwd_back = exchanges(snd2, sin, send2, recv2)
+    bwd_out = exchanges(snd3, got3, send3, recv3)
+    bwd_back = exchanges(snd4, rin, send4, recv4)
     logs[0]()
 
     def weights_of(h):
@@ -176,38 +192,45 @@
                 xtp[feature // (NY * piece), (feature // piece) % NY, pl.ds(pl.multiple_of(c * piece, piece), piece)] = (
                     turned[m * piece:(m + 1) * piece])
 
-    def part_of(color):
-        return dp.at[:, pl.ds(color * half, half)]
+    def part_of(color, q):
+        return dp.at[:, pl.ds(color * half + COLUMNS[q][0], COLUMNS[q][1])]
+
+    def p_slot(slot, q):
+        return pg.at[slot, :, pl.ds(COLUMNS[q][0], COLUMNS[q][1])]
 
     def lanes(slot):
         return xg.at[:, :, pl.ds(pl.multiple_of(slot * Q, Q), Q)]
 
-    def x_line(j):
-        k, slot = (x + j) % NX, x * 2 + core
-        peer = at(k, y, z, 0)
-        return (send(xtp.at[k], lanes(slot), x_send.at[0, j], x_recv.at[slot], peer),
-                send(part_of(0), pg.at[slot], p_send.at[0, j], p_recv.at[slot], peer))
-
-    def y_line(j):
-        k, slot = (y + j) % NY, y * 2 + core
-        peer = at(x, k, z, 1)
-        return (send(xtp.at[:, k], lanes(slot), x_send.at[1, j], x_recv.at[slot], peer),
-                send(part_of(1), pg.at[slot], p_send.at[1, j], p_recv.at[slot], peer))
+    def x_line(color, j):
+        if color == 0:
+            return send(xtp.at[(x + j) % NX], lanes(x * 2 + core), x_send.at[0, j], x_recv.at[x * 2 + core],
+                        at((x + j) % NX, y, z, 0))
+        return send(xtp.at[:, (y + j) % NY], lanes(y * 2 + core), x_send.at[1, j], x_recv.at[y * 2 + core],
+                    at(x, (y + j) % NY, z, 1))
+
+    def p_line(q):
+        def copy(color, j):
+            if color == 0:
+                return send(part_of(0, q), p_slot(x * 2 + core, q), p_send.at[q, 0, j], p_recv.at[q, x * 2 + core],
+                            at((x + j) % NX, y, z, 0))
+            return send(part_of(1, q), p_slot(y * 2 + core, q), p_send.at[q, 1, j], p_recv.at[q, y * 2 + core],
+                        at(x, (y + j) % NY, z, 1))
+        return copy
 
     def lines(what, act):
         for j in (2, 1, 3):
-            act(x_line(j)[what])
-            act(y_line(j)[what])
+            act(what(0, j))
+            act(what(1, j))
 
         @pl.when(core == 0)
         def _():
-            act(y_line(0)[what])
+            act(what(1, 0))
 
         @pl.when(core == 1)
         def _():
-            act(x_line(0)[what])
-
-    lines(0, lambda copy: copy.start())
+            act(what(0, 0))
+
+    lines(x_line, lambda copy: copy.start())
 
     @pl.when(core == 0)
     def _():
@@ -238,7 +261,8 @@
         snd1[pl.ds(g * group, group)] = states.astype(b16).reshape(group, P_SIZE, N)
 
     loop(0, H // group, local_states)
-    fwd_out[0]()
+    for one in fwd_out:
+        one[0]()
 
     scores = dot(b_nat, c_t)
 
@@ -250,19 +274,22 @@
 
     loop(0, H // group, inside)
     logs[1]()
-    fwd_out[1]()
-
-    def scan(parts, out, reverse):
+    size = P_SIZE // PIECES
+
+    def scan(parts, out, piece, reverse):
         def body(k, state):
             i = n_tm - 1 - k if reverse else k
-            out[i] = state.astype(b16).reshape(P_SIZE, N)
+            out[i, piece] = state.astype(b16).reshape(size, N)
             decay = jnp.exp(lgot[i])
-            return decay[None] * state + parts[i].astype(f32).reshape(P_SIZE // 8, 8, N)
-        lax.fori_loop(0, n_tm, body, jnp.zeros((P_SIZE // 8, 8, N), f32))
-
-    scan(got1, snd2, False)
-    fwd_back[0]()
-    fwd_back[1]()
+            return decay[None] * state + parts[i, piece].astype(f32).reshape(size // 8, 8, N)
+        lax.fori_loop(0, n_tm, body, jnp.zeros((size // 8, 8, N), f32))
+
+    for k, piece in enumerate(pieces):
+        fwd_out[k][1]()
+        scan(got1, snd2, piece, False)
+        fwd_back[k][0]()
+    for one in fwd_back:
+        one[1]()
 
     def norm_step(g):
         carried = dot(sin[pl.ds(g * group, group)].reshape(group * P_SIZE, N), c_t)
@@ -282,7 +309,8 @@
         snd3[pl.ds(g * group, group)] = states.astype(b16).reshape(group, P_SIZE, N)
 
     loop(0, H // group, norm_step)
-    bwd_out[0]()
+    for one in bwd_out:
+        one[0]()
 
     first = subs_of((2 * P_SIZE, Q)) < P_SIZE
 
@@ -300,31 +328,43 @@
         return total
 
     pair_sum = lax.fori_loop(0, H // group, pairs, jnp.zeros((Q, Q), f32)).astype(b16)
-    bwd_out[1]()
-    scan(got3, snd4, True)
-    bwd_back[0]()
+    for k, piece in enumerate(pieces):
+        bwd_out[k][1]()
+        scan(got3, snd4, piece, True)
+        bwd_back[k][0]()
     d_c = t_dot(pair_sum, b_nat) + t_dot(dl[...].reshape(hp, Q), sin[...].reshape(hp, N))
     d_b = dot(pair_sum, c_nat)
     dp[:, hp + N:hp + 2 * N] = d_c.astype(b16)
     for k in range(hp // Q):
-        out_ref[:, k * Q:(k + 1) * Q] = lot[k * Q:(k + 1) * Q].T.astype(b16)
-    bwd_back[1]()
-    d_b = d_b + t_dot(xw[...].reshape(hp, Q), rin[...].reshape(hp, N))
-    dp[:, hp:hp + N] = d_b.astype(b16)
-    for k in range(H // 2):
+        lay[:, k * Q:(k + 1) * Q] = lot[k * Q:(k + 1) * Q].T.astype(b16)
+    lay_home = pltpu.make_async_copy(lay, out_ref, o_sem)
+    lay_home.start()
+    for one in bwd_back:
+        one[1]()
+
+    def inputs_of(k):
         after = dot(rin[2 * k:2 * k + 2].reshape(2 * P_SIZE, N), b_t)
         two = [din[2 * k + i] + tail[2 * k + i:2 * k + i + 1] * after[i * P_SIZE:(i + 1) * P_SIZE] for i in range(2)]
         dp[:, k * Q:(k + 1) * Q] = (jnp.concatenate(two, axis=0) * valid).T.astype(b16)
 
-    lines(1, lambda copy: copy.start())
-
-    @pl.when(core == 0)
-    def _():
-        pltpu.make_async_copy(part_of(0), pg.at[x * 2], p_recv.at[x * 2]).start()
-
-    @pl.when(core == 1)
-    def _():
-        pltpu.make_async_copy(part_of(1), pg.at[y * 2 + 1], p_recv.at[y * 2 + 1]).start()
+    done = set()
+    for q, (off, many) in enumerate(COLUMNS):
+        for k in range(hp // Q):
+            if k not in done and any(color * half + off <= k * Q < color * half + off + many for color in range(2)):
+                done.add(k)
+                inputs_of(k)
+        if q == len(COLUMNS) - 1:
+            d_b = d_b + t_dot(xw[...].reshape(hp, Q), rin[...].reshape(hp, N))
+            dp[:, hp:hp + N] = d_b.astype(b16)
+        lines(p_line(q), lambda copy: copy.start())
+
+        @pl.when(core == 0)
+        def _():
+            pltpu.make_async_copy(part_of(0, q), p_slot(x * 2, q), p_recv.at[q, x * 2]).start()
+
+        @pl.when(core == 1)
+        def _():
+            pltpu.make_async_copy(part_of(1, q), p_slot(y * 2 + 1, q), p_recv.at[q, y * 2 + 1]).start()
 
     def e_copy(j):
         return send(rows_out.at[j], demb_ref.at[z], e_send.at[j], e_recv.at[j], ((z + 1 + j) % NZ, me))
@@ -337,71 +377,102 @@
         else:
             e_home.start()
 
+    p = (1 - core) * y + core * x
+    line = z * 2 + core
+
+    def second(j, q):
+        k = (p + 1 + j) % NX
+        peer = at((1 - core) * x + core * k, (1 - core) * k + core * y, z, core)
+        cols = pl.ds(*COLUMNS[q])
+        return send(s2.at[j, :, cols], r2.at[j, :, cols], send5.at[q, j], recv5.at[q, j], peer)
+
+    def third(j, q):
+        slot = (line + j) % (2 * NZ)
+        cols = pl.ds(*COLUMNS[q])
+        return send(s3.at[slot, :, cols], r3.at[line, :, cols], send6.at[q, j], recv6.at[q, j], at(x, y, slot // 2, slot % 2))
+
     for slot in range(8):
         pltpu.make_async_copy(xtp.at[0], lanes(slot), x_recv.at[slot]).wait()
-        pltpu.make_async_copy(part_of(0), pg.at[slot], p_recv.at[slot]).wait()
-
-    p = (1 - core) * y + core * x
-
-    def second(j):
-        k = (p + 1 + j) % NX
-        peer = at((1 - core) * x + core * k, (1 - core) * k + core * y, z, core)
-        return send(s2.at[j], r2.at[j], send5.at[j], recv5.at[j], peer)
-
-    right = pg[...].reshape(8 * Q, half)
-    for j in (1, 0, 2, 3):
-        part = dot(xg[(p + 1 + j) % NX], right)
-        if j < NX - 1:
-            s2[j] = part.astype(b16)
-            second(j).start()
-        else:
-            own[...] = part
-    for j in range(NX - 1):
-        second(j).wait_recv()
-    own[...] = (own[...] + r2[0].astype(f32) + r2[1].astype(f32) + r2[2].astype(f32)) * scale
-    line = z * 2 + core
-    for slot in range(2 * NZ):
-        s3[slot] = own[8 * slot:8 * slot + 8].astype(b16)
-
-    def third(j):
-        slot = (line + j) % (2 * NZ)
-        return send(s3.at[slot], r3.at[line], send6.at[j], recv6.at[line], at(x, y, slot // 2, slot % 2))
-
-    def third_arrival(j):
-        slot = (line + j) % (2 * NZ)
-        return send(s3.at[0], r3.at[slot], send6.at[j], recv6.at[slot], at(x, y, slot // 2, slot % 2))
-
-    for j in (8, 7, 9, 6, 10, 5, 11, 4, 12, 3, 13, 2, 14, 1, 15):
-        third(j).start()
-    r3[line] = s3[line]
-    for j in range(1, 2 * NZ):
-        third_arrival(j).wait_recv()
-    for color in range(2):
-        sums = r3[color].astype(f32)
-        for c in range(1, NZ):
-            sums = sums + r3[2 * c + color].astype(f32)
-        dw_ref[:, color * half:(color + 1) * half] = sums
-
+
+    for q, (off, many) in enumerate(COLUMNS):
+        cols = slice(off, off + many)
+        for slot in range(8):
+            pltpu.make_async_copy(part_of(0, q), p_slot(slot, q), p_recv.at[q, slot]).wait()
+        right = pg[:, :, cols].reshape(8 * Q, many)
+        for j in (1, 0, 2, 3):
+            part = dot(xg[(p + 1 + j) % NX], right)
+            if j < NX - 1:
+                s2[j, :, cols] = part.astype(b16)
+                second(j, q).start()
+            else:
+                own[:, cols] = part
+    for q, (off, many) in enumerate(COLUMNS):
+        cols = slice(off, off + many)
+        for j in range(NX - 1):
+            second(j, q).wait_recv()
+        own[:, cols] = (own[:, cols] + r2[0, :, cols].astype(f32) + r2[1, :, cols].astype(f32) + r2[2, :, cols].astype(f32)) * scale
+        for slot in range(2 * NZ):
+            s3[slot, :, cols] = own[8 * slot:8 * slot + 8, cols].astype(b16)
+        for j in (8, 7, 9, 6, 10, 5, 11, 4, 12, 3, 13, 2, 14, 1, 15):
+            third(j, q).start()
+        r3[line, :, cols] = s3[line, :, cols]
+    for q, (off, many) in enumerate(COLUMNS):
+        for j in range(1, 2 * NZ):
+            third(j, q).wait_recv()
+        for color in range(2):
+            sums = r3[color, :, off:off + many].astype(f32)
+            for c in range(1, NZ):
+                sums = sums + r3[2 * c + color, :, off:off + many].astype(f32)
+            dw_ref[:, color * half + off:color * half + off + many] = sums
+
+    lay_home.wait()
     for j in range(NZ - 1):
         a_copy(j).wait_send()
         e_copy(j).wait_send()
         e_copy(j).wait_recv()
     e_home.wait()
-    for _, _, sent in (logs, fwd_out, fwd_back, bwd_out, bwd_back):
-        sent()
-    lines(0, lambda copy: copy.wait_send())
-    lines(1, lambda copy: copy.wait_send())
-    for j in range(NX - 1):
-        second(j).wait_send()
-    for j in range(1, 2 * NZ):
-        third(j).wait_send()
+    for one in [logs] + fwd_out + fwd_back + bwd_out + bwd_back:
+        one[2]()
+    lines(x_line, lambda copy: copy.wait_send())
+    for q in range(len(COLUMNS)):
+        lines(p_line(q), lambda copy: copy.wait_send())
+        for j in range(NX - 1):
+            second(j, q).wait_send()
+        for j in range(1, 2 * NZ):
+            third(j, q).wait_send()
+
+
+def finish_kernel(*refs):
+    half = len(refs) // 4
+    ins, outs, held, sems = refs[:half], refs[half:2 * half], refs[2 * half:3 * half], refs[3 * half:]
+    loads = [pltpu.make_async_copy(a, b, sem.at[0]) for a, b, sem in zip(ins, held, sems)]
+    stores = [pltpu.make_async_copy(a, b, sem.at[1]) for a, b, sem in zip(held, outs, sems)]
+    for one in loads:
+        one.start()
+    for load, store in zip(loads, stores):
+        load.wait()
+        store.start()
+    for one in stores:
+        one.wait()
+
+
+def finish(*arrays):
+    hbm = pl.BlockSpec(memory_space=pl.ANY)
+    return pl.pallas_call(
+        finish_kernel,
+        name="finish",
+        out_shape=[jax.ShapeDtypeStruct(a.shape, a.dtype) for a in arrays],
+        in_specs=[hbm] * len(arrays),
+        out_specs=[hbm] * len(arrays),
+        scratch_shapes=[pltpu.VMEM(a.shape, a.dtype) for a in arrays] + [pltpu.SemaphoreType.DMA((2,)) for _ in arrays],
+    )(*arrays)
 
 
 def on_device(embeds, w_in, log_decay, clip_keep, clip_starts, valid_len, norm_gain, g_out):
     n_cam, t, width = embeds.shape
     d, e = w_in.shape
     n_tm = lax.axis_size("tm")
-    half, part = e // 2, d // NX // NY
+    half, part, many = e // 2, d // NX // NY, len(COLUMNS)
     scale = 1.0 / math.sqrt(n_cam * t * n_tm)
     dma = pltpu.SemaphoreType.DMA
     vmem = pl.BlockSpec(memory_space=pltpu.VMEM)
@@ -415,7 +486,7 @@
         out_shape=(jax.ShapeDtypeStruct((t, HP), b16), jax.ShapeDtypeStruct((n_cam, t, width), b16),
                    jax.ShapeDtypeStruct((part // n_cam // 2, e), f32)),
         in_specs=[smem, smem, hbm, hbm, vmem, vmem, vmem, vmem],
-        out_specs=(vmem, hbm, vmem),
+        out_specs=(hbm, hbm, vmem),
         scratch_shapes=[
             scratch(b16, n_cam, width, e), scratch(b16, t, d), scratch(f32, t, e), scratch(b16, t, e), scratch(b16, e, t),
             scratch(b16, NX, NY, part, t), scratch(b16, HP, t), scratch(f32, HP, t), scratch(f32, H, t, t),
@@ -427,14 +498,15 @@
             scratch(b16, t, e), scratch(b16, NX, part, 8 * t), scratch(b16, 8, t, half), scratch(b16, n_cam, t, width),
             scratch(b16, NX - 1, part, half), scratch(b16, NX - 1, part, half),
             scratch(b16, 2 * n_cam, part // n_cam // 2, half), scratch(b16, 2 * n_cam, part // n_cam // 2, half),
-            scratch(f32, part, half),
-            dma((n_cam,)), dma((n_cam,)), dma((n_cam,)),
-        ] + [dma((n_tm,))] * 10 + [
-            dma((2, NX)), dma((8,)), dma((2, NX)), dma((8,)), dma((n_cam,)), dma((n_cam,)),
-            dma((NX,)), dma((NX,)), dma((2 * n_cam,)), dma((2 * n_cam,)),
+            scratch(f32, part, half), scratch(b16, t, HP),
+            dma((n_cam,)), dma, dma((n_cam,)), dma((n_cam,)),
+        ] + [dma((n_tm,))] * 2 + [dma((PIECES, n_tm))] * 8 + [
+            dma((2, NX)), dma((8,)), dma((many, 2, NX)), dma((many, 8)), dma((n_cam,)), dma((n_cam,)),
+            dma((many, NX)), dma((many, NX)), dma((many, 2 * n_cam)), dma((many, 2 * n_cam)),
         ],
         compiler_params=pltpu.CompilerParams(collective_id=0, has_side_effects=True, vmem_limit_bytes=60 * 1024 * 1024),
     )(clip_starts, valid_len, embeds, w_in, log_decay, clip_keep.reshape(1, H), norm_gain.reshape(HP // Q, Q), g_out)
+    layer_out, d_embeds, d_w_in = finish(layer_out, d_embeds, d_w_in)
     return (layer_out[None], d_embeds, d_w_in)
 
 

time: 119 us -> 111 us (0.933)
  local copies, waits for them, and re-layouts: 5.27 us -> 0 us
  Pallas kernels: 112 us -> 109 us
    unnamed x3 -> x0, local copies, waits for them, and re-layouts: 5.27 us -> none
    pallas_call x1, Pallas kernels: 112 us -> 107 us  [on_device(): pl.pallas_call(functools.partial(layer_kernel, scale), name='layer', out_...]
    pallas_call x0 -> x1, Pallas kernels: none -> 2.07 us  [finish(): pl.pallas_call(finish_kernel, name='finish', out_shape=[jax.ShapeDtypeStr...]
where the time goes in v5:
time: 111 us
  Pallas kernels  109 us (98%)
  between operations  1.29 us (1%)
    pallas_call x1, Pallas kernels, on_device(): pl.pallas_call(functools.partial(layer_kernel, scale), name='layer', out_...  107 us

profile of v5, /device:TPU:1, one launch (start us, length us, event | category | flops | bytes accessed | tf_op | source)
XLA Modules:
  0.0 110.6 jit_solution(1313610025571785463)
XLA Ops:
  1.3 107.2 %layer.1 = (bf16[128,2048]{1,0:T(8,128)(2,1)}, bf16[8,128,256]{2,1,0:T(8,128)(2,1)}, f32[8,2304]{1,0:T(8,128)}) custom-call(s32[1,3]{1,0:T(1,128)} %starts_ref.1, s32[1]{0:T(128)S(6)} %copy.11.len_ref, bf16[8,128,256]{2,1,0:T(8,128)(2,1)} %emb_ref.1, bf16[2048,2304]{1,0:T(8,128)(2,1)} %w_ref.1, f32[1,32,128]{2,1,0:T(8,128)} %rate_ref.1, f32[1,32]{1,0:T(1,128)} %bitcast.4, ...), custom_call_target="tpu_custom_call" | custom-call | tf_op jit(solution)/shard_map/layer/pallas_call | solution.py:483
  108.5 2.1 %finish.1 = (bf16[128,2048]{1,0:T(8,128)(2,1)}, bf16[8,128,256]{2,1,0:T(8,128)(2,1)}, f32[8,2304]{1,0:T(8,128)}) custom-call(bf16[128,2048]{1,0:T(8,128)(2,1)} %get-tuple-element.9.refs_0_, bf16[8,128,256]{2,1,0:T(8,128)(2,1)} %get-tuple-element.10.refs_1_, f32[8,2304]{1,0:T(8,128)} %get-tuple-element.11.refs_2_), custom_call_target="tpu_custom_call" | custom-call | tf_op jit(solution)/shard_map/finish/pallas_call | solution.py:461

commit v6 on v5

--- a/solution.py
+++ b/solution.py
@@ -21,7 +21,7 @@
 MESH = pl.DeviceIdType.MESH
 NX, NY, NZ = 4, 4, 8
 PIECES = 2
-COLUMNS = ((0, 512), (512, 640))
+COLUMNS = ((0, 512), (512, 384), (896, 256))
 
 
 def at(x, y, z, core):
@@ -32,6 +32,10 @@
     return pltpu.make_async_remote_copy(
         src_ref=src, dst_ref=dst, send_sem=sem_a, recv_sem=sem_b, device_id=peer, device_id_type=MESH
     )
+
+
+def wait_for(ref, sem):
+    pltpu.make_async_copy(ref, ref, sem).wait()
 
 
 def loop(start, end, body):
@@ -114,7 +118,7 @@
 
     def a_copy(j):
         lanes = pl.ds(pl.multiple_of(z * width, width), width)
-        return send(emb_ref.at[(z + 1 + j) % NZ], xin.at[:, lanes], a_send.at[j], a_recv.at[j], ((z + 1 + j) % NZ, me))
+        return send(emb_ref.at[(z + 1 + j) % NZ], xin.at[:, lanes], a_send, a_recv.at[j], ((z + 1 + j) % NZ, me))
 
     def block(c):
         return xin.at[:, pl.ds(pl.multiple_of(c * width, width), width)]
@@ -128,22 +132,38 @@
         return (2 + 3 * i + 3 * (i // 2) + 2 * (i // 3)) % 4
 
     def exchange(src, dst, sem_a, sem_b, part=None):
-        def copy(j):
-            dx, dy = apart(j // (2 * NY)), apart((j // 2) % NY)
-            peer = (((x + dx) % NX) * NY + (y + dy) % NY) * 2 + (core + 1 + j) % 2
+        def copy(peer):
             if part is None:
-                return send(src.at[peer], dst.at[me], sem_a.at[j], sem_b.at[j], (z, peer))
-            return send(src.at[peer, part], dst.at[me, part], sem_a.at[j], sem_b.at[j], (z, peer))
-
-        def start():
-            loop(0, n_tm - 1, lambda j: copy(j).start())
+                return send(src.at[peer], dst.at[me], sem_a, sem_b, (z, peer))
+            return send(src.at[peer, part], dst.at[me, part], sem_a, sem_b, (z, peer))
+
+        def own_block():
             if part is None:
                 dst[me] = src[me]
             else:
                 dst[me, part] = src[me, part]
 
-        return (start, lambda: loop(0, n_tm - 1, lambda j: copy(j).wait_recv()),
-                lambda: loop(0, n_tm - 1, lambda j: copy(j).wait_send()))
+        def start():
+            def one(j):
+                dx, dy = apart(j // (2 * NY)), apart((j // 2) % NY)
+                copy((((x + dx) % NX) * NY + (y + dy) % NY) * 2 + (core + 1 + j) % 2).start()
+            loop(0, n_tm - 1, one)
+            own_block()
+
+        def heads_of(g):
+            for i in range(group):
+                peer = g * group + i
+
+                @pl.when(peer != me)
+                def _():
+                    copy(peer).start()
+
+        others = pl.ds(0, n_tm - 1)
+
+        def wait(ref, sem):
+            wait_for(ref.at[others] if part is None else ref.at[others, part], sem)
+
+        return start, lambda: wait(dst, sem_b), lambda: wait(src, sem_a), heads_of, own_block
 
     pieces = [pl.ds(k * (P_SIZE // PIECES), P_SIZE // PIECES) for k in range(PIECES)]
 
@@ -198,22 +218,26 @@
     def p_slot(slot, q):
         return pg.at[slot, :, pl.ds(COLUMNS[q][0], COLUMNS[q][1])]
 
-    def lanes(slot):
-        return xg.at[:, :, pl.ds(pl.multiple_of(slot * Q, Q), Q)]
-
-    def x_line(color, j):
-        if color == 0:
-            return send(xtp.at[(x + j) % NX], lanes(x * 2 + core), x_send.at[0, j], x_recv.at[x * 2 + core],
-                        at((x + j) % NX, y, z, 0))
-        return send(xtp.at[:, (y + j) % NY], lanes(y * 2 + core), x_send.at[1, j], x_recv.at[y * 2 + core],
-                    at(x, (y + j) % NY, z, 1))
+    def x_slot(slot, u):
+        return xg.at[pl.ds(2 * u, 2), :, pl.ds(pl.multiple_of(slot * Q, Q), Q)]
+
+    def x_line(u):
+        two = pl.ds(2 * u, 2)
+
+        def copy(color, j):
+            if color == 0:
+                return send(xtp.at[(x + j) % NX, two], x_slot(x * 2 + core, u), x_send.at[u], x_recv.at[u],
+                            at((x + j) % NX, y, z, 0))
+            return send(xtp.at[two, (y + j) % NY], x_slot(y * 2 + core, u), x_send.at[u], x_recv.at[u],
+                        at(x, (y + j) % NY, z, 1))
+        return copy
 
     def p_line(q):
         def copy(color, j):
             if color == 0:
-                return send(part_of(0, q), p_slot(x * 2 + core, q), p_send.at[q, 0, j], p_recv.at[q, x * 2 + core],
+                return send(part_of(0, q), p_slot(x * 2 + core, q), p_send.at[q], p_recv.at[q],
                             at((x + j) % NX, y, z, 0))
-            return send(part_of(1, q), p_slot(y * 2 + core, q), p_send.at[q, 1, j], p_recv.at[q, y * 2 + core],
+            return send(part_of(1, q), p_slot(y * 2 + core, q), p_send.at[q], p_recv.at[q],
                         at(x, (y + j) % NY, z, 1))
         return copy
 
@@ -230,15 +254,19 @@
         def _():
             act(what(0, 0))
 
-    lines(x_line, lambda copy: copy.start())
-
-    @pl.when(core == 0)
-    def _():
-        pltpu.make_async_copy(xtp.at[x], lanes(x * 2), x_recv.at[x * 2]).start()
-
-    @pl.when(core == 1)
-    def _():
-        pltpu.make_async_copy(xtp.at[:, y], lanes(y * 2 + 1), x_recv.at[y * 2 + 1]).start()
+    def x_rows(u):
+        two = pl.ds(2 * u, 2)
+        lines(x_line(u), lambda copy: copy.start())
+
+        @pl.when(core == 0)
+        def _():
+            pltpu.make_async_copy(xtp.at[x, two], x_slot(x * 2, u), x_recv.at[u]).start()
+
+        @pl.when(core == 1)
+        def _():
+            pltpu.make_async_copy(xtp.at[two, y], x_slot(y * 2 + 1, u), x_recv.at[u]).start()
+
+    x_rows(0)
 
     for k in range((hp + 2 * N) // Q):
         part = acc[:, k * Q:(k + 1) * Q]
@@ -253,6 +281,20 @@
     def rows(g, i):
         return pl.ds(pl.multiple_of((g * group + i) * P_SIZE, P_SIZE), P_SIZE)
 
+    def turn(gg):
+        return (gg + 1 + me // group) % (H // group)
+
+    def in_turns(body, piece):
+        def step(gg):
+            body(turn(gg))
+
+            @pl.when(gg > 0)
+            def _():
+                piece[3](turn(gg - 1))
+        loop(0, H // group, step)
+        piece[3](turn(H // group - 1))
+        piece[4]()
+
     def local_states(g):
         for i in range(group):
             h = g * group + i
@@ -260,8 +302,8 @@
         states = dot(xw[pl.ds(g * group, group)].reshape(group * P_SIZE, Q), b_nat)
         snd1[pl.ds(g * group, group)] = states.astype(b16).reshape(group, P_SIZE, N)
 
-    loop(0, H // group, local_states)
-    for one in fwd_out:
+    in_turns(local_states, fwd_out[0])
+    for one in fwd_out[1:]:
         one[0]()
 
     scores = dot(b_nat, c_t)
@@ -290,6 +332,7 @@
         fwd_back[k][0]()
     for one in fwd_back:
         one[1]()
+    x_rows(1)
 
     def norm_step(g):
         carried = dot(sin[pl.ds(g * group, group)].reshape(group * P_SIZE, N), c_t)
@@ -308,8 +351,8 @@
         states = dot(dl[pl.ds(g * group, group)].reshape(group * P_SIZE, Q), c_nat)
         snd3[pl.ds(g * group, group)] = states.astype(b16).reshape(group, P_SIZE, N)
 
-    loop(0, H // group, norm_step)
-    for one in bwd_out:
+    in_turns(norm_step, bwd_out[0])
+    for one in bwd_out[1:]:
         one[0]()
 
     first = subs_of((2 * P_SIZE, Q)) < P_SIZE
@@ -360,16 +403,16 @@
 
         @pl.when(core == 0)
         def _():
-            pltpu.make_async_copy(part_of(0, q), p_slot(x * 2, q), p_recv.at[q, x * 2]).start()
+            pltpu.make_async_copy(part_of(0, q), p_slot(x * 2, q), p_recv.at[q]).start()
 
         @pl.when(core == 1)
         def _():
-            pltpu.make_async_copy(part_of(1, q), p_slot(y * 2 + 1, q), p_recv.at[q, y * 2 + 1]).start()
+            pltpu.make_async_copy(part_of(1, q), p_slot(y * 2 + 1, q), p_recv.at[q]).start()
 
     def e_copy(j):
-        return send(rows_out.at[j], demb_ref.at[z], e_send.at[j], e_recv.at[j], ((z + 1 + j) % NZ, me))
-
-    e_home = pltpu.make_async_copy(rows_out.at[NZ - 1], demb_ref.at[z], e_recv.at[NZ - 1])
+        return send(rows_out.at[j], demb_ref.at[z], e_send, e_recv, ((z + 1 + j) % NZ, me))
+
+    e_home = pltpu.make_async_copy(rows_out.at[NZ - 1], demb_ref.at[z], e_recv)
     for j in (3, 2, 4, 1, 5, 0, 6, 7):
         rows_out[j] = dot_t(dp[...], wv[(z + 1 + j) % NZ]).astype(b16)
         if j < NZ - 1:
@@ -384,20 +427,20 @@
         k = (p + 1 + j) % NX
         peer = at((1 - core) * x + core * k, (1 - core) * k + core * y, z, core)
         cols = pl.ds(*COLUMNS[q])
-        return send(s2.at[j, :, cols], r2.at[j, :, cols], send5.at[q, j], recv5.at[q, j], peer)
+        return send(s2.at[j, :, cols], r2.at[j, :, cols], send5.at[q], recv5.at[q], peer)
 
     def third(j, q):
         slot = (line + j) % (2 * NZ)
         cols = pl.ds(*COLUMNS[q])
-        return send(s3.at[slot, :, cols], r3.at[line, :, cols], send6.at[q, j], recv6.at[q, j], at(x, y, slot // 2, slot % 2))
-
-    for slot in range(8):
-        pltpu.make_async_copy(xtp.at[0], lanes(slot), x_recv.at[slot]).wait()
-
-    for q, (off, many) in enumerate(COLUMNS):
+        return send(s3.at[slot, :, cols], r3.at[line, :, cols], send6.at[q], recv6.at[q], at(x, y, slot // 2, slot % 2))
+
+    for u in range(2):
+        wait_for(xg.at[pl.ds(2 * u, 2)], x_recv.at[u])
+
+    def multiply(q):
+        off, many = COLUMNS[q]
         cols = slice(off, off + many)
-        for slot in range(8):
-            pltpu.make_async_copy(part_of(0, q), p_slot(slot, q), p_recv.at[q, slot]).wait()
+        wait_for(pg.at[:, :, pl.ds(off, many)], p_recv.at[q])
         right = pg[:, :, cols].reshape(8 * Q, many)
         for j in (1, 0, 2, 3):
             part = dot(xg[(p + 1 + j) % NX], right)
@@ -406,19 +449,26 @@
                 second(j, q).start()
             else:
                 own[:, cols] = part
-    for q, (off, many) in enumerate(COLUMNS):
+
+    def add(q):
+        off, many = COLUMNS[q]
         cols = slice(off, off + many)
-        for j in range(NX - 1):
-            second(j, q).wait_recv()
+        wait_for(r2.at[:, :, pl.ds(off, many)], recv5.at[q])
         own[:, cols] = (own[:, cols] + r2[0, :, cols].astype(f32) + r2[1, :, cols].astype(f32) + r2[2, :, cols].astype(f32)) * scale
         for slot in range(2 * NZ):
             s3[slot, :, cols] = own[8 * slot:8 * slot + 8, cols].astype(b16)
         for j in (8, 7, 9, 6, 10, 5, 11, 4, 12, 3, 13, 2, 14, 1, 15):
             third(j, q).start()
         r3[line, :, cols] = s3[line, :, cols]
+
+    multiply(0)
+    for q in range(1, len(COLUMNS)):
+        multiply(q)
+        add(q - 1)
+    add(len(COLUMNS) - 1)
+    others = pl.ds(0, 2 * NZ - 1)
     for q, (off, many) in enumerate(COLUMNS):
-        for j in range(1, 2 * NZ):
-            third(j, q).wait_recv()
+        wait_for(r3.at[others, :, pl.ds(off, many)], recv6.at[q])
         for color in range(2):
             sums = r3[color, :, off:off + many].astype(f32)
             for c in range(1, NZ):
@@ -426,20 +476,18 @@
             dw_ref[:, color * half + off:color * half + off + many] = sums
 
     lay_home.wait()
-    for j in range(NZ - 1):
-        a_copy(j).wait_send()
-        e_copy(j).wait_send()
-        e_copy(j).wait_recv()
-    e_home.wait()
+    wait_for(rows_out.at[pl.ds(0, NZ - 1)], a_send)
+    wait_for(rows_out.at[pl.ds(0, NZ - 1)], e_send)
+    wait_for(demb_ref, e_recv)
     for one in [logs] + fwd_out + fwd_back + bwd_out + bwd_back:
         one[2]()
-    lines(x_line, lambda copy: copy.wait_send())
-    for q in range(len(COLUMNS)):
-        lines(p_line(q), lambda copy: copy.wait_send())
-        for j in range(NX - 1):
-            second(j, q).wait_send()
-        for j in range(1, 2 * NZ):
-            third(j, q).wait_send()
+    for u in range(2):
+        wait_for(xg.at[pl.ds(2 * u, 2), :, pl.ds(0, 7 * Q)], x_send.at[u])
+    for q, (off, many) in enumerate(COLUMNS):
+        cols = pl.ds(off, many)
+        wait_for(pg.at[pl.ds(0, 7), :, cols], p_send.at[q])
+        wait_for(s2.at[:, :, cols], send5.at[q])
+        wait_for(s3.at[others, :, cols], send6.at[q])
 
 
 def finish_kernel(*refs):
@@ -499,10 +547,10 @@
             scratch(b16, NX - 1, part, half), scratch(b16, NX - 1, part, half),
             scratch(b16, 2 * n_cam, part // n_cam // 2, half), scratch(b16, 2 * n_cam, part // n_cam // 2, half),
             scratch(f32, part, half), scratch(b16, t, HP),
-            dma((n_cam,)), dma, dma((n_cam,)), dma((n_cam,)),
-        ] + [dma((n_tm,))] * 2 + [dma((PIECES, n_tm))] * 8 + [
-            dma((2, NX)), dma((8,)), dma((many, 2, NX)), dma((many, 8)), dma((n_cam,)), dma((n_cam,)),
-            dma((many, NX)), dma((many, NX)), dma((many, 2 * n_cam)), dma((many, 2 * n_cam)),
+            dma((n_cam,)), dma, dma, dma((n_cam,)), dma, dma,
+        ] + [dma((PIECES,))] * 8 + [
+            dma((2,)), dma((2,)), dma((many,)), dma((many,)), dma, dma,
+            dma((many,)), dma((many,)), dma((many,)), dma((many,)),
         ],
         compiler_params=pltpu.CompilerParams(collective_id=0, has_side_effects=True, vmem_limit_bytes=60 * 1024 * 1024),
     )(clip_starts, valid_len, embeds, w_in, log_decay, clip_keep.reshape(1, H), norm_gain.reshape(HP // Q, Q), g_out)

time: 111 us -> 98.7 us (0.89)
  Pallas kernels: 109 us -> 97.3 us
    pallas_call x1, Pallas kernels: 107 us -> 95.2 us  [on_device(): pl.pallas_call(functools.partial(layer_kernel, scale), name='layer', out_...]
where the time goes in v6:
time: 98.7 us; the launch traced here: 98.6 us
  Pallas kernels  97.3 us (99%)
  between operations  1.29 us (1%)
    pallas_call x1, Pallas kernels, on_device(): pl.pallas_call(functools.partial(layer_kernel, scale), name='layer', out_...  95.2 us
    pallas_call x1, Pallas kernels, finish(): pl.pallas_call(finish_kernel, name='finish', out_shape=[jax.ShapeDtypeStr...  2.07 us

profile of v6, /device:TPU:1, one launch (start us, length us, event | category | flops | bytes accessed | tf_op | source)
XLA Modules:
  0.0 98.6 jit_solution(2327999524257917098)
XLA Ops:
  1.3 95.2 %layer.1 = (bf16[128,2048]{1,0:T(8,128)(2,1)}, bf16[8,128,256]{2,1,0:T(8,128)(2,1)}, f32[8,2304]{1,0:T(8,128)}) custom-call(s32[1,3]{1,0:T(1,128)} %starts_ref.1, s32[1]{0:T(128)S(6)} %copy.11.len_ref, bf16[8,128,256]{2,1,0:T(8,128)(2,1)} %emb_ref.1, bf16[2048,2304]{1,0:T(8,128)(2,1)} %w_ref.1, f32[1,32,128]{2,1,0:T(8,128)} %rate_ref.1, f32[1,32]{1,0:T(1,128)} %bitcast.4, ...), custom_call_target="tpu_custom_call" | custom-call | tf_op jit(solution)/shard_map/layer/pallas_call | solution.py:531
  96.5 2.1 %finish.1 = (bf16[128,2048]{1,0:T(8,128)(2,1)}, bf16[8,128,256]{2,1,0:T(8,128)(2,1)}, f32[8,2304]{1,0:T(8,128)}) custom-call(bf16[128,2048]{1,0:T(8,128)(2,1)} %get-tuple-element.9.refs_0_, bf16[8,128,256]{2,1,0:T(8,128)(2,1)} %get-tuple-element.10.refs_1_, f32[8,2304]{1,0:T(8,128)} %get-tuple-element.11.refs_2_), custom_call_target="tpu_custom_call" | custom-call | tf_op jit(solution)/shard_map/finish/pallas_call | solution.py:509

commit v7 on v6

--- a/solution.py
+++ b/solution.py
@@ -21,6 +21,7 @@
 MESH = pl.DeviceIdType.MESH
 NX, NY, NZ = 4, 4, 8
 PIECES = 2
+RELAY_AT = 6
 COLUMNS = ((0, 512), (512, 384), (896, 256))
 
 
@@ -52,7 +53,7 @@
                  dp, xg, pg, rows_out, s2, r2, s3, r3, own, lay,
                  w_sem, o_sem, a_send, a_recv,
                  l_send, l_recv, send1, recv1, send2, recv2, send3, recv3, send4, recv4,
-                 x_send, x_recv, p_send, p_recv, e_send, e_recv, send5, recv5, send6, recv6):
+                 x_send, x_recv, p_send, p_recv, p_near, e_send, e_recv, send5, recv5, send6, recv6):
     f32, b16 = jnp.float32, jnp.bfloat16
     me, z = lax.axis_index("tm"), lax.axis_index("cam")
     n_tm = 2 * NX * NY
@@ -131,6 +132,8 @@
     def apart(i):
         return (2 + 3 * i + 3 * (i // 2) + 2 * (i // 3)) % 4
 
+    beside = [((y + apart(k // 2)) % NY) * 2 + (core + 1 + k) % 2 for k in range(2 * NY)]
+
     def exchange(src, dst, sem_a, sem_b, part=None):
         def copy(peer):
             if part is None:
@@ -144,10 +147,17 @@
                 dst[me, part] = src[me, part]
 
         def start():
-            def one(j):
-                dx, dy = apart(j // (2 * NY)), apart((j // 2) % NY)
-                copy((((x + dx) % NX) * NY + (y + dy) % NY) * 2 + (core + 1 + j) % 2).start()
-            loop(0, n_tm - 1, one)
+            def chips_at(i):
+                line_x = ((x + apart(i)) % NX) * (2 * NY)
+                for k in range(2 * NY):
+                    peer = line_x + beside[k]
+                    if k < 2 * NY - 1:
+                        copy(peer).start()
+                    else:
+                        @pl.when(i < NX - 1)
+                        def _():
+                            copy(peer).start()
+            loop(0, NX, chips_at)
             own_block()
 
         def heads_of(g):
@@ -234,15 +244,25 @@
 
     def p_line(q):
         def copy(color, j):
+            sem = p_recv.at[q] if j == 0 else p_near.at[q, j // 2]
             if color == 0:
-                return send(part_of(0, q), p_slot(x * 2 + core, q), p_send.at[q], p_recv.at[q],
-                            at((x + j) % NX, y, z, 0))
-            return send(part_of(1, q), p_slot(y * 2 + core, q), p_send.at[q], p_recv.at[q],
-                        at(x, (y + j) % NY, z, 1))
+                return send(part_of(0, q), p_slot(x * 2 + core, q), p_send.at[q], sem, at((x + j) % NX, y, z, 0))
+            return send(part_of(1, q), p_slot(y * 2 + core, q), p_send.at[q], sem, at(x, (y + j) % NY, z, 1))
         return copy
 
-    def lines(what, act):
-        for j in (2, 1, 3):
+    spot = (1 - core) * x + core * y
+
+    def relay(q):
+        off, many = COLUMNS[q]
+        cols = pl.ds(off, many)
+        for side, step in ((0, 1), (1, 3)):
+            wait_for(pg.at[pl.ds(0, 2), :, cols], p_near.at[q, side])
+            from_chip = pg.at[pl.ds(2 * ((spot + 4 - step) % 4), 2), pl.ds(side * (Q // 2), Q // 2), cols]
+            peer = at((x + (1 - core) * step) % NX, (y + core * step) % NY, z, core)
+            send(from_chip, from_chip, p_send.at[q], p_recv.at[q], peer).start()
+
+    def lines(what, act, steps=(2, 1, 3)):
+        for j in steps:
             act(what(0, j))
             act(what(1, j))
 
@@ -265,8 +285,6 @@
         @pl.when(core == 1)
         def _():
             pltpu.make_async_copy(xtp.at[two, y], x_slot(y * 2 + 1, u), x_recv.at[u]).start()
-
-    x_rows(0)
 
     for k in range((hp + 2 * N) // Q):
         part = acc[:, k * Q:(k + 1) * Q]
@@ -305,6 +323,7 @@
     in_turns(local_states, fwd_out[0])
     for one in fwd_out[1:]:
         one[0]()
+    x_rows(0)
 
     scores = dot(b_nat, c_t)
 
@@ -332,7 +351,6 @@
         fwd_back[k][0]()
     for one in fwd_back:
         one[1]()
-    x_rows(1)
 
     def norm_step(g):
         carried = dot(sin[pl.ds(g * group, group)].reshape(group * P_SIZE, N), c_t)
@@ -354,6 +372,7 @@
     in_turns(norm_step, bwd_out[0])
     for one in bwd_out[1:]:
         one[0]()
+    x_rows(1)
 
     first = subs_of((2 * P_SIZE, Q)) < P_SIZE
 
@@ -399,7 +418,7 @@
         if q == len(COLUMNS) - 1:
             d_b = d_b + t_dot(xw[...].reshape(hp, Q), rin[...].reshape(hp, N))
             dp[:, hp:hp + N] = d_b.astype(b16)
-        lines(p_line(q), lambda copy: copy.start())
+        lines(p_line(q), lambda copy: copy.start(), (1, 3))
 
         @pl.when(core == 0)
         def _():
@@ -413,7 +432,9 @@
         return send(rows_out.at[j], demb_ref.at[z], e_send, e_recv, ((z + 1 + j) % NZ, me))
 
     e_home = pltpu.make_async_copy(rows_out.at[NZ - 1], demb_ref.at[z], e_recv)
-    for j in (3, 2, 4, 1, 5, 0, 6, 7):
+    for n, j in enumerate((3, 2, 4, 1, 5, 0, 6, 7)):
+        if n == RELAY_AT:
+            relay(0)
         rows_out[j] = dot_t(dp[...], wv[(z + 1 + j) % NZ]).astype(b16)
         if j < NZ - 1:
             e_copy(j).start()
@@ -440,7 +461,7 @@
     def multiply(q):
         off, many = COLUMNS[q]
         cols = slice(off, off + many)
-        wait_for(pg.at[:, :, pl.ds(off, many)], p_recv.at[q])
+        wait_for(pg.at[pl.ds(0, 4), :, pl.ds(off, many)], p_recv.at[q])
         right = pg[:, :, cols].reshape(8 * Q, many)
         for j in (1, 0, 2, 3):
             part = dot(xg[(p + 1 + j) % NX], right)
@@ -461,6 +482,8 @@
             third(j, q).start()
         r3[line, :, cols] = s3[line, :, cols]
 
+    for q in range(1, len(COLUMNS)):
+        relay(q)
     multiply(0)
     for q in range(1, len(COLUMNS)):
         multiply(q)
@@ -549,7 +572,7 @@
             scratch(f32, part, half), scratch(b16, t, HP),
             dma((n_cam,)), dma, dma, dma((n_cam,)), dma, dma,
         ] + [dma((PIECES,))] * 8 + [
-            dma((2,)), dma((2,)), dma((many,)), dma((many,)), dma, dma,
+            dma((2,)), dma((2,)), dma((many,)), dma((many,)), dma((many, 2)), dma, dma,
             dma((many,)), dma((many,)), dma((many,)), dma((many,)),
         ],
         compiler_params=pltpu.CompilerParams(collective_id=0, has_side_effects=True, vmem_limit_bytes=60 * 1024 * 1024),

time: 98.7 us -> 96.2 us (0.975)
  Pallas kernels: 97.3 us -> 94.8 us
    pallas_call x1, Pallas kernels: 95.2 us -> 92.7 us  [on_device(): pl.pallas_call(functools.partial(layer_kernel, scale), name='layer', out_...]
where the time goes in v7:
time: 96.2 us; the launch traced here: 96 us
  Pallas kernels  94.8 us (99%)
  between operations  1.29 us (1%)
    pallas_call x1, Pallas kernels, on_device(): pl.pallas_call(functools.partial(layer_kernel, scale), name='layer', out_...  92.7 us
    pallas_call x1, Pallas kernels, finish(): pl.pallas_call(finish_kernel, name='finish', out_shape=[jax.ShapeDtypeStr...  2.07 us

profile of v7, /device:TPU:1, one launch (start us, length us, event | category | flops | bytes accessed | tf_op | source)
XLA Modules:
  0.0 96.0 jit_solution(4316102514781755940)
XLA Ops:
  1.3 92.7 %layer.1 = (bf16[128,2048]{1,0:T(8,128)(2,1)}, bf16[8,128,256]{2,1,0:T(8,128)(2,1)}, f32[8,2304]{1,0:T(8,128)}) custom-call(s32[1,3]{1,0:T(1,128)} %starts_ref.1, s32[1]{0:T(128)S(6)} %copy.11.len_ref, bf16[8,128,256]{2,1,0:T(8,128)(2,1)} %emb_ref.1, bf16[2048,2304]{1,0:T(8,128)(2,1)} %w_ref.1, f32[1,32,128]{2,1,0:T(8,128)} %rate_ref.1, f32[1,32]{1,0:T(1,128)} %bitcast.4, ...), custom_call_target="tpu_custom_call" | custom-call | tf_op jit(solution)/shard_map/layer/pallas_call | solution.py:554
  94.0 2.1 %finish.1 = (bf16[128,2048]{1,0:T(8,128)(2,1)}, bf16[8,128,256]{2,1,0:T(8,128)(2,1)}, f32[8,2304]{1,0:T(8,128)}) custom-call(bf16[128,2048]{1,0:T(8,128)(2,1)} %get-tuple-element.9.refs_0_, bf16[8,128,256]{2,1,0:T(8,128)(2,1)} %get-tuple-element.10.refs_1_, f32[8,2304]{1,0:T(8,128)} %get-tuple-element.11.refs_2_), custom_call_target="tpu_custom_call" | custom-call | tf_op jit(solution)/shard_map/finish/pallas_call | solution.py:532

commit v8 on v7

--- a/solution.py
+++ b/solution.py
@@ -46,12 +46,12 @@
     lax.fori_loop(start, end, step, 0)
 
 
-def layer_kernel(scale, starts_ref, len_ref, emb_ref, w_ref, rate_ref, keep_ref, gain_ref, g_ref,
+def layer_kernel(scale, starts_ref, len_ref, emb_ref, w_ref, rate_hbm, keep_ref, gain_hbm, g_hbm,
                  out_ref, demb_ref, dw_ref,
                  wv, xin, acc, proj, xt, xtp, gt, gain, wts, cum, tail, lift, tot,
                  xw, mix, yin, dt, dl, din, lot, lg, lgot, snd1, got1, snd2, sin, snd3, got3, snd4, rin,
-                 dp, xg, pg, rows_out, s2, r2, s3, r3, own, lay,
-                 w_sem, o_sem, a_send, a_recv,
+                 dp, xg, pg, rows_out, s2, r2, s3, r3, own, lay, rate_ref, gain_ref, g_ref,
+                 w_sem, o_sem, in_sem, a_send, a_recv,
                  l_send, l_recv, send1, recv1, send2, recv2, send3, recv3, send4, recv4,
                  x_send, x_recv, p_send, p_recv, p_near, e_send, e_recv, send5, recv5, send6, recv6):
     f32, b16 = jnp.float32, jnp.bfloat16
@@ -61,12 +61,16 @@
     hp = H * P_SIZE
     width = emb_ref.shape[2]
     half = dp.shape[1] // 2
-    group = 4
+    group = 8
 
     def w_copy(j):
         c = (z + NZ - 1 - j) % NZ
         return pltpu.make_async_copy(w_ref.at[pl.ds(pl.multiple_of(c * width, width), width)], wv.at[c], w_sem.at[j])
 
+    loads = [pltpu.make_async_copy(a, b, in_sem.at[k]) for k, (a, b) in enumerate(
+        ((rate_hbm, rate_ref), (gain_hbm, gain_ref), (g_hbm, g_ref)))]
+    for one in loads:
+        one.start()
     barrier = pltpu.get_barrier_semaphore()
 
     def greet(peer):
@@ -100,6 +104,7 @@
         is_start = is_start | (here == starts_ref[0, k])
     keep_log = jnp.log(keep_ref[...])
     keep_col = jnp.sum(jnp.where(lanes_of((H, H)) == subs_of((H, H)), keep_log, 0.0), axis=1, keepdims=True)
+    loads[0].wait()
     rates = rate_ref[0] + jnp.where(is_start, keep_col, 0.0)
     upper = (subs_of((Q, Q)) <= lanes_of((Q, Q)))
     running = jnp.dot(rates, upper.astype(f32), precision=lax.Precision.HIGHEST, preferred_element_type=f32)
@@ -192,6 +197,9 @@
         wts[h] = jnp.where(upper, jnp.exp(jnp.where(upper, row - row.T, 0.0)), 0.0)
 
     loop(0, H, weights_of)
+
+    loads[1].wait()
+    loads[2].wait()
 
     def columns_of(k):
         part = pl.ds(pl.multiple_of(k * Q, Q), Q)
@@ -556,7 +564,7 @@
         name="layer",
         out_shape=(jax.ShapeDtypeStruct((t, HP), b16), jax.ShapeDtypeStruct((n_cam, t, width), b16),
                    jax.ShapeDtypeStruct((part // n_cam // 2, e), f32)),
-        in_specs=[smem, smem, hbm, hbm, vmem, vmem, vmem, vmem],
+        in_specs=[smem, smem, hbm, hbm, hbm, vmem, hbm, hbm],
         out_specs=(hbm, hbm, vmem),
         scratch_shapes=[
             scratch(b16, n_cam, width, e), scratch(b16, t, d), scratch(f32, t, e), scratch(b16, t, e), scratch(b16, e, t),
@@ -570,7 +578,8 @@
             scratch(b16, NX - 1, part, half), scratch(b16, NX - 1, part, half),
             scratch(b16, 2 * n_cam, part // n_cam // 2, half), scratch(b16, 2 * n_cam, part // n_cam // 2, half),
             scratch(f32, part, half), scratch(b16, t, HP),
-            dma((n_cam,)), dma, dma, dma((n_cam,)), dma, dma,
+            scratch(f32, 1, H, t), scratch(f32, HP // Q, Q), scratch(b16, 1, t, HP),
+            dma((n_cam,)), dma, dma((3,)), dma, dma((n_cam,)), dma, dma,
         ] + [dma((PIECES,))] * 8 + [
             dma((2,)), dma((2,)), dma((many,)), dma((many,)), dma((many, 2)), dma, dma,
             dma((many,)), dma((many,)), dma((many,)), dma((many,)),

time: 96.2 us -> 95.2 us (0.990)
  Pallas kernels: 94.8 us -> 93.7 us
    pallas_call x1, Pallas kernels: 92.7 us -> 91.7 us  [on_device(): pl.pallas_call(functools.partial(layer_kernel, scale), name='layer', out_...]
where the time goes in v8:
time: 95.2 us; the launch traced here: 95 us
  Pallas kernels  93.7 us (98%)
  between operations  1.29 us (1%)
    pallas_call x1, Pallas kernels, on_device(): pl.pallas_call(functools.partial(layer_kernel, scale), name='layer', out_...  91.7 us
    pallas_call x1, Pallas kernels, finish(): pl.pallas_call(finish_kernel, name='finish', out_shape=[jax.ShapeDtypeStr...  2.07 us

profile of v8, /device:TPU:1, one launch (start us, length us, event | category | flops | bytes accessed | tf_op | source)
XLA Modules:
  0.0 95.0 jit_solution(7992190790749866205)
XLA Ops:
  1.3 91.7 %layer.1 = (bf16[128,2048]{1,0:T(8,128)(2,1)}, bf16[8,128,256]{2,1,0:T(8,128)(2,1)}, f32[8,2304]{1,0:T(8,128)}) custom-call(s32[1,3]{1,0:T(1,128)} %starts_ref.1, s32[1]{0:T(128)S(6)} %copy.11.len_ref, bf16[8,128,256]{2,1,0:T(8,128)(2,1)} %emb_ref.1, bf16[2048,2304]{1,0:T(8,128)(2,1)} %w_ref.1, f32[1,32,128]{2,1,0:T(8,128)} %rate_hbm.1, f32[1,32]{1,0:T(1,128)} %bitcast.4, ...), custom_call_target="tpu_custom_call" | custom-call | tf_op jit(solution)/shard_map/layer/pallas_call | solution.py:562
  93.0 2.1 %finish.1 = (bf16[128,2048]{1,0:T(8,128)(2,1)}, bf16[8,128,256]{2,1,0:T(8,128)(2,1)}, f32[8,2304]{1,0:T(8,128)}) custom-call(bf16[128,2048]{1,0:T(8,128)(2,1)} %get-tuple-element.9.refs_0_, bf16[8,128,256]{2,1,0:T(8,128)(2,1)} %get-tuple-element.10.refs_1_, f32[8,2304]{1,0:T(8,128)} %get-tuple-element.11.refs_2_), custom_call_target="tpu_custom_call" | custom-call | tf_op jit(solution)/shard_map/finish/pallas_call | solution.py:540

commit v9 on v8

--- a/solution.py
+++ b/solution.py
@@ -346,12 +346,15 @@
     size = P_SIZE // PIECES
 
     def scan(parts, out, piece, reverse):
-        def body(k, state):
-            i = n_tm - 1 - k if reverse else k
-            out[i, piece] = state.astype(b16).reshape(size, N)
-            decay = jnp.exp(lgot[i])
-            return decay[None] * state + parts[i, piece].astype(f32).reshape(size // 8, 8, N)
-        lax.fori_loop(0, n_tm, body, jnp.zeros((size // 8, 8, N), f32))
+        def body(m, state):
+            for n in range(8):
+                k = m * 8 + n
+                i = n_tm - 1 - k if reverse else k
+                out[i, piece] = state.astype(b16).reshape(size, N)
+                decay = jnp.exp(lgot[i])
+                state = decay[None] * state + parts[i, piece].astype(f32).reshape(size // 8, 8, N)
+            return state
+        lax.fori_loop(0, n_tm // 8, body, jnp.zeros((size // 8, 8, N), f32))
 
     for k, piece in enumerate(pieces):
         fwd_out[k][1]()

time: 95.2 us -> 95.1 us (level)
  no operation moved by 1% of the time
where the time goes in v9:
time: 95.1 us; the launch traced here: 95 us
  Pallas kernels  93.7 us (99%)
  between operations  1.29 us (1%)
    pallas_call x1, Pallas kernels, on_device(): pl.pallas_call(functools.partial(layer_kernel, scale), name='layer', out_...  91.6 us
    pallas_call x1, Pallas kernels, finish(): pl.pallas_call(finish_kernel, name='finish', out_shape=[jax.ShapeDtypeStr...  2.07 us

profile of v9, /device:TPU:1, one launch (start us, length us, event | category | flops | bytes accessed | tf_op | source)
XLA Modules:
  0.0 95.0 jit_solution(4525656087088905443)
XLA Ops:
  1.3 91.6 %layer.1 = (bf16[128,2048]{1,0:T(8,128)(2,1)}, bf16[8,128,256]{2,1,0:T(8,128)(2,1)}, f32[8,2304]{1,0:T(8,128)}) custom-call(s32[1,3]{1,0:T(1,128)} %starts_ref.1, s32[1]{0:T(128)S(6)} %copy.11.len_ref, bf16[8,128,256]{2,1,0:T(8,128)(2,1)} %emb_ref.1, bf16[2048,2304]{1,0:T(8,128)(2,1)} %w_ref.1, f32[1,32,128]{2,1,0:T(8,128)} %rate_hbm.1, f32[1,32]{1,0:T(1,128)} %bitcast.4, ...), custom_call_target="tpu_custom_call" | custom-call | tf_op jit(solution)/shard_map/layer/pallas_call | solution.py:565
  92.9 2.1 %finish.1 = (bf16[128,2048]{1,0:T(8,128)(2,1)}, bf16[8,128,256]{2,1,0:T(8,128)(2,1)}, f32[8,2304]{1,0:T(8,128)}) custom-call(bf16[128,2048]{1,0:T(8,128)(2,1)} %get-tuple-element.9.refs_0_, bf16[8,128,256]{2,1,0:T(8,128)(2,1)} %get-tuple-element.10.refs_1_, f32[8,2304]{1,0:T(8,128)} %get-tuple-element.11.refs_2_), custom_call_target="tpu_custom_call" | custom-call | tf_op jit(solution)/shard_map/finish/pallas_call | solution.py:543
